TPU v7x, 32 devices: a whole 2x2x4 slice. The times are simulated.
32 devices in a mesh: row: 8 (over z, x), col: 4 (over y, core).
Axes of the slice: x: 2, y: 2, z: 4, core: 2. Of those that a mesh axis runs over, the one named last changes fastest.
Arguments:
- pixels: bfloat16 [512, 512, 384], P('row', 'col'), may hold values from -40 to 40, as said below
- start: float32 [384, 64], replicated, may hold values from -0.3125 to 0.3125
Outputs:
- mean: float32 [384], replicated
- projector: float32 [384, 384], replicated
- scores: float32 [64, 512, 512], P(None, 'row', 'col')
Inputs may be any that keep to these rules, and one draw needn't show every extreme that they name: `pixels`: Real-valued features.
All inputs are finite; a program needn't handle non-finite values.
Results may differ from a plain program's by a relative error of at most 0.0029.
Values may be sent and summed in bfloat16 or wider, within the bound.
No kernel may reach another device: no remote copies, remote signals or barrier semaphores. Data moves between devices by JAX's collectives and lax.ppermute only.
A program may use at most 64 MiB of HBM per device.

v0:
```python
import functools

import jax
import jax.numpy as jnp
from jax import lax
from jax.experimental import pallas as pl
from jax.experimental.pallas import tpu as pltpu
from jax.sharding import PartitionSpec as P


ITERS = 4
LANES = 128
AHEAD = 16
CHUNK = 4

GAUSS = (0.0625, 0.25, 0.375, 0.25, 0.0625)


WIDTH = 2
HALO_ROWS = 16


def edges(axis, first, last):
    up = [(i, i + 1) for i in range(lax.axis_size(axis) - 1)]
    down = [(j, i) for i, j in up]
    return lax.ppermute(last, axis, up), lax.ppermute(first, axis, down)


def edge_weight(first, count, total):
    position = first + jnp.arange(count, dtype=jnp.int32)
    weight = jnp.zeros((count,), jnp.float32)
    for offset in range(5):
        inside = (position + offset - 2 >= 0) & (position + offset - 2 < total)
        weight = weight + GAUSS[offset] * inside.astype(jnp.float32)
    return weight


def column_taps(count):
    out = jnp.arange(count, dtype=jnp.int32)[:, None]
    k = jnp.arange(count + HALO_ROWS, dtype=jnp.int32)[None, :]
    beside = k - count
    place = jnp.where(k < count, k, jnp.where(beside < WIDTH, beside - WIDTH, count + beside - WIDTH))
    place = jnp.where(beside < 2 * WIDTH, place, -count)
    taps = jnp.zeros((count, count + HALO_ROWS), jnp.float32)
    for offset in range(5):
        taps = jnp.where(place == out + offset - 2, GAUSS[offset], taps)
    return taps.astype(jnp.bfloat16)


def cascade(c):
    for _ in range(4):
        c = [p + q for p, q in zip(c, c[1:])]
    return c


def correlate(s, gram, ends):
    wide = s.shape[1] - LANES
    over = (((0,), (0,)), ((), ()))
    last = jnp.concatenate([s[:, wide:], jnp.ones((s.shape[0], LANES), jnp.bfloat16)], axis=1)
    gram[...] += lax.dot_general(s[:, :wide], s[:, :wide], over, preferred_element_type=jnp.float32)
    ends[...] += lax.dot_general(s, last, over, preferred_element_type=jnp.float32)


def inner_kernel(
    pixels, left, right, taps, col_scale, smooth_hbm, gram, ends, kept,
    source, across, rounded, smooth, in_sem, out_sem,
):
    tile_rows, tile_cols, feat = pixels.shape
    group = 8
    groups = tile_rows // group
    strip = tile_cols // group
    count = lambda g: group if g + 1 < groups else group - 2 * WIDTH

    def fetch(g):
        rows = pl.ds(g * group, group)
        there = source.at[rows, pl.ds(0, tile_cols), :]
        return pltpu.make_async_copy(pixels.at[rows], there, in_sem.at[g])

    def send(g):
        rows = pl.ds(g * group + WIDTH, count(g))
        return pltpu.make_async_copy(smooth.at[rows], smooth_hbm.at[rows], out_sem.at[g])

    for g in range(groups):
        fetch(g).start()
    source[:, tile_cols:, :] = jnp.zeros((tile_rows, HALO_ROWS, feat), jnp.bfloat16)
    source[:, tile_cols : tile_cols + WIDTH, :] = left[...]
    source[:, tile_cols + WIDTH : tile_cols + 2 * WIDTH, :] = right[...]
    gram[...] = jnp.zeros_like(gram)
    ends[...] = jnp.zeros_like(ends)

    def horizontal(g, q):
        across[g % 4, q] = jnp.dot(taps[...], source[group * g + 4 + q], preferred_element_type=jnp.float32)

    def vertical(g, i):
        at = slice(i * strip, (i + 1) * strip)
        scale = col_scale[at, :] * GAUSS[0]
        for f in range(feat // LANES):
            lanes = slice(f * LANES, (f + 1) * LANES)
            held = []
            for r in range(4 + count(g)):
                v = across[(g - 1) % 4, 4 + r, at, lanes] if r < 4 else across[g % 4, r - 4, at, lanes]
                for k in range(4):
                    if k == len(held):
                        held.append(v)
                        break
                    v, held[k] = v + held[k], v
                else:
                    v = (v * scale).astype(jnp.bfloat16)
                    smooth[g * group + WIDTH + r - 4, at, lanes] = v
                    rounded[g % 2, r - 4, at, lanes] = v

    fetch(0).wait()
    for q in range(4, group):
        horizontal(-1, q)
    fetch(1).wait()
    for q in range(group):
        horizontal(0, q)
    for g in range(groups + 1):
        if g + 2 < groups:
            fetch(g + 2).wait()
        for q in range(group):
            if g + 1 < groups and q < count(g + 1):
                horizontal(g + 1, q)
            if g < groups:
                vertical(g, q)
            if g > 0 and q % CHUNK == CHUNK - 1 and q < count(g - 1):
                rows = rounded[(g - 1) % 2, q - CHUNK + 1 : q + 1]
                correlate(rows.reshape(CHUNK * tile_cols, feat), gram, ends)
        if g < groups:
            send(g).start()
    own = 2 * WIDTH
    kept[:own] = source[:own]
    kept[own:] = source[tile_rows - own :]
    for g in range(groups):
        send(g).wait()


def edge_kernel(
    row_scale, above, below, kept, taps, col_scale, gram_in, ends_in, rounded, packed, beside, across, gram, ends
):
    tile_rows = row_scale.shape[0]
    _, tile_cols, feat = rounded.shape
    own = 2 * WIDTH
    side = own + WIDTH
    beside[:, tile_cols:, :] = jnp.zeros((2 * WIDTH, HALO_ROWS, feat), jnp.bfloat16)
    beside[:WIDTH, 0 : tile_cols + 2 * WIDTH, :] = above[...]
    beside[WIDTH:, 0 : tile_cols + 2 * WIDTH, :] = below[...]
    sources = [beside.at[k] for k in range(WIDTH)] + [kept.at[k] for k in range(2 * own)]
    sources += [beside.at[k] for k in range(WIDTH, 2 * WIDTH)]
    for k, source in enumerate(sources):
        across[k] = jnp.dot(taps[...], source[...], preferred_element_type=jnp.float32)
    strip = 16
    for k, first in enumerate((0, tile_rows - WIDTH)):
        for i in range(tile_cols // strip):
            at = slice(i * strip, (i + 1) * strip)
            scales = [col_scale[at, :] * row_scale[first + r] for r in range(WIDTH)]
            for f in range(feat // LANES):
                lanes = slice(f * LANES, (f + 1) * LANES)
                c = [across[side * k + r, at, lanes] for r in range(side)]
                for r, total in enumerate(cascade(c)):
                    rounded[WIDTH * k + r, at, lanes] = (total * scales[r]).astype(jnp.bfloat16)
    gram[...] = gram_in[...]
    ends[...] = ends_in[...]
    correlate(rounded[...].reshape(2 * WIDTH * tile_cols, feat), gram, ends)
    row = lax.broadcasted_iota(jnp.int32, (LANES, LANES), 0)
    col = lax.broadcasted_iota(jnp.int32, (LANES, LANES), 1)
    n = feat // LANES
    at = 0
    for i in range(n):
        for j in range(i, n):
            rows = slice(i * LANES, (i + 1) * LANES)
            block = ends[rows, :LANES] if j == n - 1 else gram[rows, j * LANES : (j + 1) * LANES]
            if i == j:
                piece = ends[rows, LANES:]
                block = jnp.where((col == 0) & (row > 0), piece, block)
                block = jnp.where((col == 1) & (row == LANES - 1), piece[0:1, :], block)
            packed[at * LANES : (at + 1) * LANES, :] = block
            at += 1


def smooth_and_gram(pixels, left, right, row_edges, taps, row_scale, col_scale):
    tile_rows, tile_cols, feat = pixels.shape
    n = feat // LANES
    wide = feat - LANES
    vmem = pl.BlockSpec(memory_space=pltpu.VMEM)
    hbm = pl.BlockSpec(memory_space=pltpu.HBM)
    smem = pl.BlockSpec(memory_space=pltpu.SMEM)
    pixels = pltpu.with_memory_space_constraint(pixels, pltpu.HBM)
    above, below = row_edges
    width = tile_cols + HALO_ROWS
    smoothed, gram, ends, kept = pl.pallas_call(
        inner_kernel,
        out_shape=(
            pltpu.HBM(pixels.shape, jnp.bfloat16),
            jax.ShapeDtypeStruct((wide, wide), jnp.float32),
            jax.ShapeDtypeStruct((feat, 2 * LANES), jnp.float32),
            jax.ShapeDtypeStruct((4 * WIDTH, width, feat), jnp.bfloat16),
        ),
        in_specs=[hbm, vmem, vmem, vmem, vmem],
        out_specs=(hbm, vmem, vmem, vmem),
        scratch_shapes=[
            pltpu.VMEM((tile_rows, width, feat), jnp.bfloat16),
            pltpu.VMEM((4, 8, tile_cols, feat), jnp.float32),
            pltpu.VMEM((2, 8, tile_cols, feat), jnp.bfloat16),
            pltpu.VMEM(pixels.shape, jnp.bfloat16),
            pltpu.SemaphoreType.DMA((tile_rows // 8,)),
            pltpu.SemaphoreType.DMA((tile_rows // 8,)),
        ],
        compiler_params=pltpu.CompilerParams(vmem_limit_bytes=40 << 20),
        cost_estimate=pl.CostEstimate(flops=10**10, bytes_accessed=3 * 10**7, transcendentals=0),
        name="smooth_inner",
    )(pixels, left, right, taps, col_scale)
    edge_rows, packed = pl.pallas_call(
        edge_kernel,
        out_shape=(
            jax.ShapeDtypeStruct((2 * WIDTH, tile_cols, feat), jnp.bfloat16),
            jax.ShapeDtypeStruct((n * (n + 1) // 2 * LANES, LANES), jnp.float32),
        ),
        in_specs=[smem] + [vmem] * 7,
        out_specs=(vmem, vmem),
        scratch_shapes=[
            pltpu.VMEM((2 * WIDTH, width, feat), jnp.bfloat16),
            pltpu.VMEM((6 * WIDTH, tile_cols, feat), jnp.float32),
            pltpu.VMEM((wide, wide), jnp.float32),
            pltpu.VMEM((feat, 2 * LANES), jnp.float32),
        ],
        compiler_params=pltpu.CompilerParams(vmem_limit_bytes=40 << 20),
        cost_estimate=pl.CostEstimate(flops=10**9, bytes_accessed=10**6, transcendentals=0),
        name="smooth_edges",
    )(row_scale, above, below, kept, taps, col_scale, gram, ends)
    return smoothed, edge_rows, packed


def all_sum(values):
    axes = ("row", "col")
    rows, cols = lax.axis_size("row"), lax.axis_size("col")
    if rows & (rows - 1) or cols & (cols - 1) or cols < 2:
        return lax.psum(values, axes)

    def pairs(row_bit, col_bit):
        return [(r * cols + c, (r ^ row_bit) * cols + (c ^ col_bit)) for r in range(rows) for c in range(cols)]

    core = pairs(0, 1)
    odd = lax.axis_index("col") % 2
    half = values.shape[0] // 2
    mine = lax.dynamic_slice_in_dim(values, odd * half, half)
    other = lax.dynamic_slice_in_dim(values, (1 - odd) * half, half)
    kept = mine + lax.ppermute(other, axes, core)
    row_steps = [pairs(1 << k, 0) for k in range(rows.bit_length() - 1)]
    col_steps = [pairs(0, 1 << k) for k in range(1, cols.bit_length() - 1)]
    order = row_steps[:1] + col_steps + row_steps[1:]
    turned = order[len(order) // 2 :] + order[: len(order) // 2]
    quarter = half // 2
    a, b = kept[:quarter], kept[quarter:]
    for first, second in zip(order, turned):
        got_a = lax.ppermute(a, axes, first)
        got_b = lax.ppermute(b, axes, second)
        a = a + got_a
        b = b + got_b
    kept = jnp.concatenate([a, b])
    got = lax.ppermute(kept, axes, core)
    return jnp.where(odd == 0, jnp.concatenate([kept, got]), jnp.concatenate([got, kept]))


def inverse_factor(a):
    n = a.shape[0]
    row = lax.broadcasted_iota(jnp.int32, (n, n), 0)
    col = lax.broadcasted_iota(jnp.int32, (n, n), 1)
    work = jnp.concatenate([a, (row == col).astype(jnp.float32)], axis=1)
    blocks = [work[8 * i : 8 * i + 8] for i in range(n // 8)]
    sub = lax.broadcasted_iota(jnp.int32, (8, 2 * n), 0)
    ahead = min(AHEAD, n)
    pivots = []
    for j0 in range(0, n, ahead):
        cols = [
            {i: jnp.broadcast_to(blocks[i][:, j : j + 1], (8, 2 * n)) for i in range(j // 8, n // 8)}
            for j in range(j0, j0 + ahead)
        ]
        for k in range(ahead):
            j = j0 + k
            top = j // 8
            s = j - 8 * top
            recip = 1.0 / jnp.broadcast_to(cols[k][top][s : s + 1], (8, 2 * n))
            pivots.append(recip)
            factor = dict(cols[k])
            factor[top] = jnp.where(sub > s, factor[top], 0.0)
            for m in range(k + 1, ahead):
                other = (j0 + m) // 8
                t = j0 + m - 8 * other
                scaled = jnp.broadcast_to(cols[k][other][t : t + 1], (8, 2 * n)) * recip
                for i in cols[m]:
                    cols[m][i] = cols[m][i] - factor[i] * scaled
            line = jnp.broadcast_to(blocks[top][s : s + 1], (8, 2 * n)) * recip
            for i in range(top, n // 8):
                blocks[i] = blocks[i] - factor[i] * line
    out = []
    for i in range(n // 8):
        scale = pivots[8 * i]
        for s in range(1, 8):
            scale = jnp.where(sub == s, pivots[8 * i + s], scale)
        out.append((blocks[i] * lax.sqrt(scale))[:, n:])
    return jnp.concatenate(out, axis=0)


def thirds(x):
    high = x.astype(jnp.bfloat16)
    rest = x - high.astype(jnp.float32)
    middle = rest.astype(jnp.bfloat16)
    return high, middle, (rest - middle.astype(jnp.float32)).astype(jnp.bfloat16)


def dot(a, b, contract):
    return lax.dot_general(a, b, (contract, ((), ())), preferred_element_type=jnp.float32)


def dot_thirds(a, b):
    m = a[0].shape[0]
    one = dot(jnp.concatenate(a, axis=0), b[0], ((1,), (0,)))
    two = dot(jnp.concatenate(a[:2], axis=0), b[1], ((1,), (0,)))
    low = one[2 * m :] + two[m:] + dot(a[0], b[2], ((1,), (0,)))
    return one[:m] + (one[m : 2 * m] + two[:m] + low)


def gram_thirds(y):
    m = y[0].shape[0]
    stack = jnp.concatenate(y, axis=0)
    p = dot(stack, stack, ((1,), (1,)))
    part = lambda i, j: p[i * m : (i + 1) * m, j * m : (j + 1) * m]
    return part(0, 0) + ((part(0, 1) + part(1, 0)) + (part(1, 1) + (part(0, 2) + part(2, 0))))


def components_kernel(
    count, packed, start, edge_rows, smooth_hbm, mean_out, proj_out, scores_hbm,
    cov, cov_thirds, subspace, basis_b, shift, smooth, scores, in_sem, out_sem,
):
    feat = cov.shape[0]
    n = feat // LANES
    rank = start.shape[1]
    tile_rows = smooth.shape[0]
    inner = pl.ds(WIDTH, tile_rows - 2 * WIDTH)
    fetch = pltpu.make_async_copy(smooth_hbm.at[inner], smooth.at[inner], in_sem)
    fetch.start()
    row = lax.broadcasted_iota(jnp.int32, (LANES, LANES), 0)
    col = lax.broadcasted_iota(jnp.int32, (LANES, LANES), 1)
    inv = 1.0 / count
    index = {}
    for i in range(n):
        for j in range(i, n):
            index[i, j] = len(index)
    block = lambda i, j: packed[index[i, j] * LANES : (index[i, j] + 1) * LANES, :]
    means, mean_cols, diag = [], [], []
    for i in range(n):
        b = block(i, i)
        bt = b.T
        first = jnp.broadcast_to(b[LANES - 1 : LANES, 1:2], (LANES, LANES))
        m = jnp.where(row > 0, jnp.broadcast_to(b[:, 0:1], (LANES, LANES)), first) * inv
        means.append(m.T[0:1, :])
        mean_cols.append(m)
        diag.append(jnp.where(row <= col, b, bt))
    mean = jnp.concatenate(means, axis=1)
    mean_out[...] = mean[0]
    for i in range(n):
        for j in range(i, n):
            g = diag[i] if i == j else block(i, j)
            c = g * inv - mean_cols[i] * means[j]
            cov[i * LANES : (i + 1) * LANES, j * LANES : (j + 1) * LANES] = c
            if i != j:
                cov[j * LANES : (j + 1) * LANES, i * LANES : (i + 1) * LANES] = c.T
    split = thirds(cov[...])
    for k in range(3):
        cov_thirds[k] = split[k]
    product = lambda parts: dot_thirds(parts, [cov_thirds[k] for k in range(3)])
    subspace[...] = product(thirds(start[...].T))

    @pl.loop(0, ITERS - 1)
    def _(step):
        parts = thirds(subspace[...])
        z = product(parts)
        lower = inverse_factor(gram_thirds(parts))
        subspace[...] = dot_thirds(thirds(lower), thirds(z))

    parts = thirds(subspace[...])
    lower = inverse_factor(gram_thirds(parts))
    y = dot_thirds(thirds(lower), parts)
    basis = y
    b = thirds(basis)
    left = jnp.concatenate([b[0], b[0], b[1], b[1], b[0], b[2]], axis=0)
    right = jnp.concatenate([b[0], b[1], b[0], b[1], b[2], b[0]], axis=0)
    proj_out[...] = dot(left, right, ((0,), (0,)))
    rounded = basis.astype(jnp.bfloat16)
    basis_b[...] = rounded
    total = jnp.sum(rounded.astype(jnp.float32) * mean, axis=1, keepdims=True)
    shift[...] = jnp.broadcast_to(total, (rank, LANES))
    fetch.wait()
    smooth[:WIDTH] = edge_rows[:WIDTH]
    smooth[tile_rows - WIDTH :] = edge_rows[WIDTH:]

    def send(g):
        here = scores.at[g].reshape(rank, 8, smooth.shape[1])
        return pltpu.make_async_copy(here, scores_hbm.at[:, pl.ds(8 * g, 8), :], out_sem.at[g])

    groups = tile_rows // 8

    @pl.loop(0, groups, unroll=2)
    def _(g):
        for h in range(8):
            s = dot(basis_b[...], smooth[8 * g + h], ((1,), (1,)))
            scores[g, pl.ds(h, rank, stride=8), :] = s - shift[...]
        send(g).start()

    for g in range(groups):
        send(g).wait()


def components(packed, start, edge_rows, smoothed, count):
    tile_rows, tile_cols, feat = smoothed.shape
    rank = start.shape[1]
    vmem = pl.BlockSpec(memory_space=pltpu.VMEM)
    hbm = pl.BlockSpec(memory_space=pltpu.HBM)
    return pl.pallas_call(
        functools.partial(components_kernel, count),
        out_shape=(
            jax.ShapeDtypeStruct((feat,), jnp.float32),
            jax.ShapeDtypeStruct((feat, feat), jnp.float32),
            pltpu.HBM((rank, tile_rows, tile_cols), jnp.float32),
        ),
        in_specs=[vmem, vmem, vmem, hbm],
        out_specs=(vmem, vmem, hbm),
        scratch_shapes=[
            pltpu.VMEM((feat, feat), jnp.float32),
            pltpu.VMEM((3, feat, feat), jnp.bfloat16),
            pltpu.VMEM((rank, feat), jnp.float32),
            pltpu.VMEM((rank, feat), jnp.bfloat16),
            pltpu.VMEM((rank, LANES), jnp.float32),
            pltpu.VMEM((tile_rows, tile_cols, feat), jnp.bfloat16),
            pltpu.VMEM((tile_rows // 8, rank * 8, tile_cols), jnp.float32),
            pltpu.SemaphoreType.DMA,
            pltpu.SemaphoreType.DMA((tile_rows // 8,)),
        ],
        compiler_params=pltpu.CompilerParams(vmem_limit_bytes=40 << 20),
        cost_estimate=pl.CostEstimate(flops=10**9, bytes_accessed=10**7, transcendentals=0),
        name="components",
    )(packed, start, edge_rows, pltpu.with_memory_space_constraint(smoothed, pltpu.HBM))


def local(pixels, start):
    tile_rows, tile_cols, _ = pixels.shape
    rows_total = tile_rows * lax.axis_size("row")
    cols_total = tile_cols * lax.axis_size("col")
    left, right = edges("col", pixels[:, :WIDTH], pixels[:, tile_cols - WIDTH :])
    wider = lambda rows: jnp.concatenate([pixels[rows], left[rows], right[rows]], axis=1)
    row_edges = edges("row", wider(slice(0, WIDTH)), wider(slice(tile_rows - WIDTH, tile_rows)))
    row_scale = GAUSS[0] / edge_weight(lax.axis_index("row") * tile_rows, tile_rows, rows_total)
    col_scale = 1.0 / edge_weight(lax.axis_index("col") * tile_cols, tile_cols, cols_total)
    col_scale = jnp.broadcast_to(col_scale[:, None], (tile_cols, LANES))
    smoothed, edge_rows, packed = smooth_and_gram(
        pixels, left, right, row_edges, column_taps(tile_cols), row_scale, col_scale
    )
    packed = all_sum(packed)
    mean, projector, scores = components(packed, start, edge_rows, smoothed, float(rows_total * cols_total))
    return (mean, projector, scores)


def solution(mesh):
    in_specs = (P("row", "col", None), P())
    out_specs = (P(), P(), P(None, "row", "col"))
    return jax.shard_map(local, mesh=mesh, in_specs=in_specs, out_specs=out_specs, check_vma=False)
```

profile of v0, /device:TPU:0, one launch (start us, length us, event | category | flops | bytes accessed | tf_op | source)
XLA Modules:
  0.0 71.6 jit_solution(8203821158464598680)
XLA Ops:
  0.6 1.3 %fusion.11 = (bf16[64,2,384]{2,1,0:T(2,128)(2,1)S(1)}, bf16[64,2,384]{2,1,0:T(2,128)(2,1)S(1)}) fusion(bf16[64,128,384]{2,1,0:T(8,128)(2,1)} %pixels.1), kind=kLoop, calls=%fused_computation.41 | loop fusion | bytes 393216 | tf_op jit(solution)/shard_map/slice | solution.py:450
  1.9 2.4 %collective-permute-start = (bf16[64,2,384]{2,1,0:T(2,128)(2,1)S(1)}, bf16[64,2,384]{2,1,0:T(2,128)(2,1)S(1)}, u32[]{:S(2)}, u32[]{:S(2)}) collective-permute-start(bf16[64,2,384]{2,1,0:T(2,128)(2,1)S(1)} %get-tuple-element.17), channel_id=1, source_target_pairs={{0,1},{1,2},{2,3},{4,5},{5,6},{6,7},{8,9},{9,10},{10,11},{12,13},{... | collective-permute-start | bytes 294920 | tf_op jit(solution)/shard_map/ppermute | solution.py:26
  4.3 1.3 %collective-permute-start.1 = (bf16[64,2,384]{2,1,0:T(2,128)(2,1)S(1)}, bf16[64,2,384]{2,1,0:T(2,128)(2,1)S(1)}, u32[]{:S(2)}, u32[]{:S(2)}) collective-permute-start(bf16[64,2,384]{2,1,0:T(2,128)(2,1)S(1)} %get-tuple-element.18), channel_id=1, source_target_pairs={{1,0},{2,1},{3,2},{5,4},{6,5},{7,6},{9,8},{10,9},{11,10},{13,12},{... | collective-permute-start | bytes 294920 | tf_op jit(solution)/shard_map/ppermute | solution.py:26
  5.7 1.1 %fusion.10 = (bf16[2,128,384]{2,1,0:T(8,128)(2,1)S(1)}, bf16[2,128,384]{2,1,0:T(8,128)(2,1)S(1)}) fusion(bf16[64,128,384]{2,1,0:T(8,128)(2,1)} %pixels.1), kind=kLoop, calls=%fused_computation.40 | loop fusion | bytes 786432 | tf_op jit(solution)/shard_map/slice | solution.py:451
  6.8 0.1 select_convert_fusion.taps
  7.0 2.7 %collective-permute-done.1.right = bf16[64,2,384]{2,1,0:T(2,128)(2,1)S(1)} collective-permute-done((bf16[64,2,384]{2,1,0:T(2,128)(2,1)S(1)}, bf16[64,2,384]{2,1,0:T(2,128)(2,1)S(1)}, u32[]{:S(2)}, u32[]{:S(2)}) %collective-permute-start.1) | collective-permute-done | bytes 98336 | tf_op jit(solution)/shard_map/ppermute | solution.py:26
  9.7 3.4 %collective-permute-start.2 = (bf16[2,132,384]{2,1,0:T(8,128)(2,1)S(1)}, bf16[2,132,384]{2,1,0:T(8,128)(2,1)S(1)}, u32[]{:S(2)}, u32[]{:S(2)}) collective-permute-start(bf16[2,132,384]{2,1,0:T(8,128)(2,1)S(1)} %pad_maximum_fusion), channel_id=1, source_target_pairs={{0,4},{4,8},{8,12},{12,16},{16,20},{20,24},{24,28},{1,5},{5,9},{9,... | collective-permute-start | bytes 608264 | tf_op jit(solution)/shard_map/ppermute | solution.py:26
  13.1 1.3 %collective-permute-start.3 = (bf16[2,132,384]{2,1,0:T(8,128)(2,1)S(1)}, bf16[2,132,384]{2,1,0:T(8,128)(2,1)S(1)}, u32[]{:S(2)}, u32[]{:S(2)}) collective-permute-start(bf16[2,132,384]{2,1,0:T(8,128)(2,1)S(1)} %pad_maximum_fusion.1), channel_id=1, source_target_pairs={{4,0},{8,4},{12,8},{16,12},{20,16},{24,20},{28,24},{5,1},{9,5},{13... | collective-permute-start | bytes 608264 | tf_op jit(solution)/shard_map/ppermute | solution.py:26
  14.4 0.1 broadcast_in_dim.29.col_scale
  14.5 9.6 %smooth_inner.1 = (bf16[64,128,384]{2,1,0:T(8,128)(2,1)}, f32[256,256]{1,0:T(8,128)S(1)}, f32[384,256]{1,0:T(8,128)S(1)}, bf16[8,144,384]{2,1,0:T(8,128)(2,1)S(1)}) custom-call(bf16[64,128,384]{2,1,0:T(8,128)(2,1)} %pixels.1, bf16[64,2,384]{2,1,0:T(2,128)(2,1)S(1)} %collective-permute-done.left, bf16[64,2,384]{2,1,0:T(2,128)(2,1)S(1)} %collective-permute-done.1.right, ...), custom_call_target="tpu_custom_call" | custom-call | flops 10000000000 | bytes 30000000 | tf_op jit(solution)/shard_map/smooth_inner/pallas_call | solution.py:191
  24.1 0.0 copy-start
  24.1 1.6 %smooth_edges.1 = (bf16[4,128,384]{2,1,0:T(8,128)(2,1)S(1)}, f32[768,128]{1,0:T(8,128)S(1)}) custom-call(f32[64]{0:T(128)S(1)} %fusion.9.row_scale, bf16[2,132,384]{2,1,0:T(8,128)(2,1)S(1)} %collective-permute-done.2.above, bf16[2,132,384]{2,1,0:T(8,128)(2,1)S(1)} %collective-permute-done.3.below, bf16[8,144,384]{2,1,0:T(8,128)(2,1)S(1)} %get-tuple-element.9.kept, ...), custom_call_target="tpu_custom_call" | custom-call | flops 1000000000 | bytes 1000000 | tf_op jit(solution)/shard_map/smooth_edges/pallas_call | solution.py:213
  25.7 3.0 %collective-permute-start.4 = (f32[384,128]{1,0:T(8,128)S(1)}, f32[384,128]{1,0:T(8,128)S(1)}, u32[]{:S(2)}, u32[]{:S(2)}) collective-permute-start(f32[384,128]{1,0:T(8,128)S(1)} %constant_dynamic-slice_fusion), channel_id=1, source_target_pairs={{0,1},{1,0},{2,3},{3,2},{4,5},{5,4},{6,7},{7,6},{8,9},{9,8},{10,11... | collective-permute-start | bytes 589832 | tf_op jit(solution)/shard_map/ppermute | solution.py:248
  28.7 1.1 %collective-permute-done.4 = f32[384,128]{1,0:T(8,128)S(1)} collective-permute-done((f32[384,128]{1,0:T(8,128)S(1)}, f32[384,128]{1,0:T(8,128)S(1)}, u32[]{:S(2)}, u32[]{:S(2)}) %collective-permute-start.4) | collective-permute-done | bytes 196640 | tf_op jit(solution)/shard_map/ppermute | solution.py:248
  29.9 2.4 %collective-permute-start.5 = (f32[192,128]{1,0:T(8,128)S(1)}, f32[192,128]{1,0:T(8,128)S(1)}, u32[]{:S(2)}, u32[]{:S(2)}) collective-permute-start(f32[192,128]{1,0:T(8,128)S(1)} %get-tuple-element.21), channel_id=1, source_target_pairs={{0,4},{1,5},{2,6},{3,7},{4,0},{5,1},{6,2},{7,3},{8,12},{9,13},{10,... | collective-permute-start | bytes 294920 | tf_op jit(solution)/shard_map/ppermute | solution.py:256
  32.3 1.6 %collective-permute-start.9 = (f32[192,128]{1,0:T(8,128)S(1)}, f32[192,128]{1,0:T(8,128)S(1)}, u32[]{:S(2)}, u32[]{:S(2)}) collective-permute-start(f32[192,128]{1,0:T(8,128)S(1)} %get-tuple-element.22), channel_id=1, source_target_pairs={{0,8},{1,9},{2,10},{3,11},{4,12},{5,13},{6,14},{7,15},{8,0},{9,1},... | collective-permute-start | bytes 294920 | tf_op jit(solution)/shard_map/ppermute | solution.py:257
  33.9 1.8 %collective-permute-done.5 = f32[192,128]{1,0:T(8,128)S(1)} collective-permute-done((f32[192,128]{1,0:T(8,128)S(1)}, f32[192,128]{1,0:T(8,128)S(1)}, u32[]{:S(2)}, u32[]{:S(2)}) %collective-permute-start.5) | collective-permute-done | bytes 98336 | tf_op jit(solution)/shard_map/ppermute | solution.py:256
  35.6 1.5 %collective-permute-done.9 = f32[192,128]{1,0:T(8,128)S(1)} collective-permute-done((f32[192,128]{1,0:T(8,128)S(1)}, f32[192,128]{1,0:T(8,128)S(1)}, u32[]{:S(2)}, u32[]{:S(2)}) %collective-permute-start.9) | collective-permute-done | bytes 98336 | tf_op jit(solution)/shard_map/ppermute | solution.py:257
  37.1 0.6 collective-permute-start.6
  37.7 2.6 %collective-permute-start.10 = (f32[192,128]{1,0:T(8,128)S(1)}, f32[192,128]{1,0:T(8,128)S(1)}, u32[]{:S(2)}, u32[]{:S(2)}) collective-permute-start(f32[192,128]{1,0:T(8,128)S(1)} %get-tuple-element.20), channel_id=1, source_target_pairs={{0,16},{1,17},{2,18},{3,19},{4,20},{5,21},{6,22},{7,23},{8,24},{9,... | collective-permute-start | bytes 294920 | tf_op jit(solution)/shard_map/ppermute | solution.py:257
  40.3 1.5 %collective-permute-done.6 = f32[192,128]{1,0:T(8,128)S(1)} collective-permute-done((f32[192,128]{1,0:T(8,128)S(1)}, f32[192,128]{1,0:T(8,128)S(1)}, u32[]{:S(2)}, u32[]{:S(2)}) %collective-permute-start.6) | collective-permute-done | bytes 98336 | tf_op jit(solution)/shard_map/ppermute | solution.py:256
  41.8 1.6 %collective-permute-start.7 = (f32[192,128]{1,0:T(8,128)S(1)}, f32[192,128]{1,0:T(8,128)S(1)}, u32[]{:S(2)}, u32[]{:S(2)}) collective-permute-start(f32[192,128]{1,0:T(8,128)S(1)} %add.257), channel_id=1, source_target_pairs={{0,8},{1,9},{2,10},{3,11},{4,12},{5,13},{6,14},{7,15},{8,0},{9,1},... | collective-permute-start | bytes 294920 | tf_op jit(solution)/shard_map/ppermute | solution.py:256
  43.5 1.5 %collective-permute-start.11 = (f32[192,128]{1,0:T(8,128)S(1)}, f32[192,128]{1,0:T(8,128)S(1)}, u32[]{:S(2)}, u32[]{:S(2)}) collective-permute-start(f32[192,128]{1,0:T(8,128)S(1)} %add.261), channel_id=1, source_target_pairs={{0,4},{1,5},{2,6},{3,7},{4,0},{5,1},{6,2},{7,3},{8,12},{9,13},{10,... | collective-permute-start | bytes 294920 | tf_op jit(solution)/shard_map/ppermute | solution.py:257
  45.0 1.5 %collective-permute-done.7 = f32[192,128]{1,0:T(8,128)S(1)} collective-permute-done((f32[192,128]{1,0:T(8,128)S(1)}, f32[192,128]{1,0:T(8,128)S(1)}, u32[]{:S(2)}, u32[]{:S(2)}) %collective-permute-start.7) | collective-permute-done | bytes 98336 | tf_op jit(solution)/shard_map/ppermute | solution.py:256
  46.5 2.6 %collective-permute-start.8 = (f32[192,128]{1,0:T(8,128)S(1)}, f32[192,128]{1,0:T(8,128)S(1)}, u32[]{:S(2)}, u32[]{:S(2)}) collective-permute-start(f32[192,128]{1,0:T(8,128)S(1)} %add.258), channel_id=1, source_target_pairs={{0,16},{1,17},{2,18},{3,19},{4,20},{5,21},{6,22},{7,23},{8,24},{9,... | collective-permute-start | bytes 294920 | tf_op jit(solution)/shard_map/ppermute | solution.py:256
  49.2 0.8 %collective-permute-start.12 = (f32[192,128]{1,0:T(8,128)S(1)}, f32[192,128]{1,0:T(8,128)S(1)}, u32[]{:S(2)}, u32[]{:S(2)}) collective-permute-start(f32[192,128]{1,0:T(8,128)S(1)} %add.262), channel_id=1, source_target_pairs={{0,2},{1,3},{2,0},{3,1},{4,6},{5,7},{6,4},{7,5},{8,10},{9,11},{10,... | collective-permute-start | bytes 294920 | tf_op jit(solution)/shard_map/ppermute | solution.py:257
  50.0 2.1 %collective-permute-done.8 = f32[192,128]{1,0:T(8,128)S(1)} collective-permute-done((f32[192,128]{1,0:T(8,128)S(1)}, f32[192,128]{1,0:T(8,128)S(1)}, u32[]{:S(2)}, u32[]{:S(2)}) %collective-permute-start.8) | collective-permute-done | bytes 98336 | tf_op jit(solution)/shard_map/ppermute | solution.py:256
  52.1 1.7 %collective-permute-done.12 = f32[192,128]{1,0:T(8,128)S(1)} collective-permute-done((f32[192,128]{1,0:T(8,128)S(1)}, f32[192,128]{1,0:T(8,128)S(1)}, u32[]{:S(2)}, u32[]{:S(2)}) %collective-permute-start.12) | collective-permute-done | bytes 98336 | tf_op jit(solution)/shard_map/ppermute | solution.py:257
  53.9 0.1 collective-permute-start.13
  54.0 0.1 copy.5.start
  54.1 1.3 %collective-permute-done.13 = f32[384,128]{1,0:T(8,128)S(1)} collective-permute-done((f32[384,128]{1,0:T(8,128)S(1)}, f32[384,128]{1,0:T(8,128)S(1)}, u32[]{:S(2)}, u32[]{:S(2)}) %collective-permute-start.13) | collective-permute-done | bytes 196640 | tf_op jit(solution)/shard_map/ppermute | solution.py:261
  55.4 16.0 %components.1 = (f32[384]{0:T(512)}, f32[384,384]{1,0:T(8,128)}, f32[64,64,128]{2,1,0:T(8,128)}) custom-call(f32[768,128]{1,0:T(8,128)S(1)} %maximum_select_fusion.packed, f32[384,64]{1,0:T(8,128)S(1)} %copy.5.start, bf16[4,128,384]{2,1,0:T(8,128)(2,1)S(1)} %get-tuple-element.13.edge_rows, bf16[64,128,384]{2,1,0:T(8,128)(2,1)} %get-tuple-element.14.smooth_hbm), custom_call_target="tpu_custom_call" | custom-call | flops 1000000000 | bytes 10000000 | tf_op jit(solution)/shard_map/components/pallas_call | solution.py:420
  (27 shorter events, 0.3 us)
Async XLA Ops:
  1.9 5.0 %collective-permute-start = (bf16[64,2,384]{2,1,0:T(2,128)(2,1)S(1)}, bf16[64,2,384]{2,1,0:T(2,128)(2,1)S(1)}, u32[]{:S(2)}, u32[]{:S(2)}) collective-permute-start(bf16[64,2,384]{2,1,0:T(2,128)(2,1)S(1)} %get-tuple-element.17), channel_id=1, source_target_pairs={{0,1},{1,2},{2,3},{4,5},{5,6},{6,7},{8,9},{9,10},{10,11},{12,13},{... | collective-permute-start | bytes 294920 | tf_op jit(solution)/shard_map/ppermute | solution.py:26
  4.3 5.3 %collective-permute-start.1 = (bf16[64,2,384]{2,1,0:T(2,128)(2,1)S(1)}, bf16[64,2,384]{2,1,0:T(2,128)(2,1)S(1)}, u32[]{:S(2)}, u32[]{:S(2)}) collective-permute-start(bf16[64,2,384]{2,1,0:T(2,128)(2,1)S(1)} %get-tuple-element.18), channel_id=1, source_target_pairs={{1,0},{2,1},{3,2},{5,4},{6,5},{7,6},{9,8},{10,9},{11,10},{13,12},{... | collective-permute-start | bytes 294920 | tf_op jit(solution)/shard_map/ppermute | solution.py:26
  9.7 14.4 %collective-permute-start.2 = (bf16[2,132,384]{2,1,0:T(8,128)(2,1)S(1)}, bf16[2,132,384]{2,1,0:T(8,128)(2,1)S(1)}, u32[]{:S(2)}, u32[]{:S(2)}) collective-permute-start(bf16[2,132,384]{2,1,0:T(8,128)(2,1)S(1)} %pad_maximum_fusion), channel_id=1, source_target_pairs={{0,4},{4,8},{8,12},{12,16},{16,20},{20,24},{24,28},{1,5},{5,9},{9,... | collective-permute-start | bytes 608264 | tf_op jit(solution)/shard_map/ppermute | solution.py:26
  13.1 11.0 %collective-permute-start.3 = (bf16[2,132,384]{2,1,0:T(8,128)(2,1)S(1)}, bf16[2,132,384]{2,1,0:T(8,128)(2,1)S(1)}, u32[]{:S(2)}, u32[]{:S(2)}) collective-permute-start(bf16[2,132,384]{2,1,0:T(8,128)(2,1)S(1)} %pad_maximum_fusion.1), channel_id=1, source_target_pairs={{4,0},{8,4},{12,8},{16,12},{20,16},{24,20},{28,24},{5,1},{9,5},{13... | collective-permute-start | bytes 608264 | tf_op jit(solution)/shard_map/ppermute | solution.py:26
  24.1 29.9 %copy-start = (f32[384,64]{0,1:T(8,128)S(1)}, f32[384,64]{0,1:T(8,128)}, u32[]{:S(2)}) copy-start(f32[384,64]{0,1:T(8,128)} %param.3) | copy-start | bytes 294916
  25.7 4.1 %collective-permute-start.4 = (f32[384,128]{1,0:T(8,128)S(1)}, f32[384,128]{1,0:T(8,128)S(1)}, u32[]{:S(2)}, u32[]{:S(2)}) collective-permute-start(f32[384,128]{1,0:T(8,128)S(1)} %constant_dynamic-slice_fusion), channel_id=1, source_target_pairs={{0,1},{1,0},{2,3},{3,2},{4,5},{5,4},{6,7},{7,6},{8,9},{9,8},{10,11... | collective-permute-start | bytes 589832 | tf_op jit(solution)/shard_map/ppermute | solution.py:248
  29.9 5.8 %collective-permute-start.5 = (f32[192,128]{1,0:T(8,128)S(1)}, f32[192,128]{1,0:T(8,128)S(1)}, u32[]{:S(2)}, u32[]{:S(2)}) collective-permute-start(f32[192,128]{1,0:T(8,128)S(1)} %get-tuple-element.21), channel_id=1, source_target_pairs={{0,4},{1,5},{2,6},{3,7},{4,0},{5,1},{6,2},{7,3},{8,12},{9,13},{10,... | collective-permute-start | bytes 294920 | tf_op jit(solution)/shard_map/ppermute | solution.py:256
  32.3 4.8 %collective-permute-start.9 = (f32[192,128]{1,0:T(8,128)S(1)}, f32[192,128]{1,0:T(8,128)S(1)}, u32[]{:S(2)}, u32[]{:S(2)}) collective-permute-start(f32[192,128]{1,0:T(8,128)S(1)} %get-tuple-element.22), channel_id=1, source_target_pairs={{0,8},{1,9},{2,10},{3,11},{4,12},{5,13},{6,14},{7,15},{8,0},{9,1},... | collective-permute-start | bytes 294920 | tf_op jit(solution)/shard_map/ppermute | solution.py:257
  37.1 4.7 %collective-permute-start.6 = (f32[192,128]{1,0:T(8,128)S(1)}, f32[192,128]{1,0:T(8,128)S(1)}, u32[]{:S(2)}, u32[]{:S(2)}) collective-permute-start(f32[192,128]{1,0:T(8,128)S(1)} %get-tuple-element.19), channel_id=1, source_target_pairs={{0,2},{1,3},{2,0},{3,1},{4,6},{5,7},{6,4},{7,5},{8,10},{9,11},{10,... | collective-permute-start | bytes 294920 | tf_op jit(solution)/shard_map/ppermute | solution.py:256
  37.7 5.7 %collective-permute-start.10 = (f32[192,128]{1,0:T(8,128)S(1)}, f32[192,128]{1,0:T(8,128)S(1)}, u32[]{:S(2)}, u32[]{:S(2)}) collective-permute-start(f32[192,128]{1,0:T(8,128)S(1)} %get-tuple-element.20), channel_id=1, source_target_pairs={{0,16},{1,17},{2,18},{3,19},{4,20},{5,21},{6,22},{7,23},{8,24},{9,... | collective-permute-start | bytes 294920 | tf_op jit(solution)/shard_map/ppermute | solution.py:257
  41.8 4.7 %collective-permute-start.7 = (f32[192,128]{1,0:T(8,128)S(1)}, f32[192,128]{1,0:T(8,128)S(1)}, u32[]{:S(2)}, u32[]{:S(2)}) collective-permute-start(f32[192,128]{1,0:T(8,128)S(1)} %add.257), channel_id=1, source_target_pairs={{0,8},{1,9},{2,10},{3,11},{4,12},{5,13},{6,14},{7,15},{8,0},{9,1},... | collective-permute-start | bytes 294920 | tf_op jit(solution)/shard_map/ppermute | solution.py:256
  43.5 5.7 %collective-permute-start.11 = (f32[192,128]{1,0:T(8,128)S(1)}, f32[192,128]{1,0:T(8,128)S(1)}, u32[]{:S(2)}, u32[]{:S(2)}) collective-permute-start(f32[192,128]{1,0:T(8,128)S(1)} %add.261), channel_id=1, source_target_pairs={{0,4},{1,5},{2,6},{3,7},{4,0},{5,1},{6,2},{7,3},{8,12},{9,13},{10,... | collective-permute-start | bytes 294920 | tf_op jit(solution)/shard_map/ppermute | solution.py:257
  46.5 5.6 %collective-permute-start.8 = (f32[192,128]{1,0:T(8,128)S(1)}, f32[192,128]{1,0:T(8,128)S(1)}, u32[]{:S(2)}, u32[]{:S(2)}) collective-permute-start(f32[192,128]{1,0:T(8,128)S(1)} %add.258), channel_id=1, source_target_pairs={{0,16},{1,17},{2,18},{3,19},{4,20},{5,21},{6,22},{7,23},{8,24},{9,... | collective-permute-start | bytes 294920 | tf_op jit(solution)/shard_map/ppermute | solution.py:256
  49.2 4.7 %collective-permute-start.12 = (f32[192,128]{1,0:T(8,128)S(1)}, f32[192,128]{1,0:T(8,128)S(1)}, u32[]{:S(2)}, u32[]{:S(2)}) collective-permute-start(f32[192,128]{1,0:T(8,128)S(1)} %add.262), channel_id=1, source_target_pairs={{0,2},{1,3},{2,0},{3,1},{4,6},{5,7},{6,4},{7,5},{8,10},{9,11},{10,... | collective-permute-start | bytes 294920 | tf_op jit(solution)/shard_map/ppermute | solution.py:257
  53.9 1.5 %collective-permute-start.13 = (f32[384,128]{1,0:T(8,128)S(1)}, f32[384,128]{1,0:T(8,128)S(1)}, u32[]{:S(2)}, u32[]{:S(2)}) collective-permute-start(f32[384,128]{1,0:T(8,128)S(1)} %pad_maximum_fusion.2), channel_id=1, source_target_pairs={{0,1},{1,0},{2,3},{3,2},{4,5},{5,4},{6,7},{7,6},{8,9},{9,8},{10,11... | collective-permute-start | bytes 589832 | tf_op jit(solution)/shard_map/ppermute | solution.py:261
where the time goes:
time: 71.8 us; the launch traced here: 71.6 us
  Pallas kernels  27.1 us (38%)
  starting transfers between devices  25.3 us (35%)
  waiting for transfers between devices  15.1 us (21%)
  local copies, waits for them, and re-layouts  2.6 us (4%)
  between operations  1.07 us (1%)
    pallas_call x1, Pallas kernels, components(): pl.pallas_call(functools.partial(components_kernel, count), out_shape=(ja...  16 us
    pallas_call x1, Pallas kernels, smooth_and_gram(): pl.pallas_call(inner_kernel, out_shape=(pltpu.HBM(pixels.shape, jnp.bfloa...  9.55 us
    ppermute x4, starting transfers between devices, edges(): return (lax.ppermute(last, axis, up), lax.ppermute(first, axis, down))  8.39 us
    ppermute x4, starting transfers between devices, all_sum(): got_a = lax.ppermute(a, axes, first)  7.31 us
    ppermute x4, waiting for transfers between devices, all_sum(): got_a = lax.ppermute(a, axes, first)  6.91 us
    ppermute x4, starting transfers between devices, all_sum(): got_b = lax.ppermute(b, axes, second)  6.45 us
    ppermute x4, waiting for transfers between devices, all_sum(): got_b = lax.ppermute(b, axes, second)  3.2 us
    ppermute x1, starting transfers between devices, all_sum(): kept = mine + lax.ppermute(other, axes, core)  3.03 us
  transfers between devices with their start and end apart: 14, of which 9 were waited for; matrix products, arithmetic and copies ran while one was open for 2% of the time, Pallas kernels for 13%

commit v1 on v0

--- a/solution.py
+++ b/solution.py
@@ -63,7 +63,7 @@
 
 def inner_kernel(
     pixels, left, right, taps, col_scale, smooth_hbm, gram, ends, kept,
-    source, across, rounded, smooth, in_sem, out_sem,
+    source, across, smooth, in_sem, out_sem,
 ):
     tile_rows, tile_cols, feat = pixels.shape
     group = 8
@@ -107,7 +107,6 @@
                 else:
                     v = (v * scale).astype(jnp.bfloat16)
                     smooth[g * group + WIDTH + r - 4, at, lanes] = v
-                    rounded[g % 2, r - 4, at, lanes] = v
 
     fetch(0).wait()
     for q in range(4, group):
@@ -124,7 +123,8 @@
             if g < groups:
                 vertical(g, q)
             if g > 0 and q % CHUNK == CHUNK - 1 and q < count(g - 1):
-                rows = rounded[(g - 1) % 2, q - CHUNK + 1 : q + 1]
+                first = (g - 1) * group + WIDTH + q - CHUNK + 1
+                rows = smooth[first : first + CHUNK]
                 correlate(rows.reshape(CHUNK * tile_cols, feat), gram, ends)
         if g < groups:
             send(g).start()
@@ -201,7 +201,6 @@
         scratch_shapes=[
             pltpu.VMEM((tile_rows, width, feat), jnp.bfloat16),
             pltpu.VMEM((4, 8, tile_cols, feat), jnp.float32),
-            pltpu.VMEM((2, 8, tile_cols, feat), jnp.bfloat16),
             pltpu.VMEM(pixels.shape, jnp.bfloat16),
             pltpu.SemaphoreType.DMA((tile_rows // 8,)),
             pltpu.SemaphoreType.DMA((tile_rows // 8,)),
@@ -401,7 +400,7 @@
 
     groups = tile_rows // 8
 
-    @pl.loop(0, groups, unroll=2)
+    @pl.loop(0, groups, unroll=8)
     def _(g):
         for h in range(8):
             s = dot(basis_b[...], smooth[8 * g + h], ((1,), (1,)))

time: 71.8 us -> 71.2 us (level)
  no operation moved by 1% of the time
where the time goes in v1:
time: 71.2 us; the launch traced here: 71 us
  Pallas kernels  26.5 us (37%)
  starting transfers between devices  25.2 us (35%)
  waiting for transfers between devices  15.1 us (21%)
  local copies, waits for them, and re-layouts  2.6 us (4%)
  between operations  1.07 us (2%)
    pallas_call x1, Pallas kernels, components(): pl.pallas_call(functools.partial(components_kernel, count), out_shape=(ja...  15.7 us
    pallas_call x1, Pallas kernels, smooth_and_gram(): pl.pallas_call(inner_kernel, out_shape=(pltpu.HBM(pixels.shape, jnp.bfloa...  9.26 us
    ppermute x4, starting transfers between devices, edges(): return (lax.ppermute(last, axis, up), lax.ppermute(first, axis, down))  8.39 us
    ppermute x4, starting transfers between devices, all_sum(): got_a = lax.ppermute(a, axes, first)  7.32 us
    ppermute x4, waiting for transfers between devices, all_sum(): got_a = lax.ppermute(a, axes, first)  6.91 us
    ppermute x4, starting transfers between devices, all_sum(): got_b = lax.ppermute(b, axes, second)  6.43 us
    ppermute x4, waiting for transfers between devices, all_sum(): got_b = lax.ppermute(b, axes, second)  3.2 us
    ppermute x1, starting transfers between devices, all_sum(): kept = mine + lax.ppermute(other, axes, core)  3.03 us
  transfers between devices with their start and end apart: 14, of which 9 were waited for; matrix products, arithmetic and copies ran while one was open for 2% of the time, Pallas kernels for 13%

profile of v1, /device:TPU:0, one launch (start us, length us, event | category | flops | bytes accessed | tf_op | source)
XLA Modules:
  0.0 71.0 jit_solution(10572306376378233130)
XLA Ops:
  0.6 1.3 %fusion.11 = (bf16[64,2,384]{2,1,0:T(2,128)(2,1)S(1)}, bf16[64,2,384]{2,1,0:T(2,128)(2,1)S(1)}) fusion(bf16[64,128,384]{2,1,0:T(8,128)(2,1)} %pixels.1), kind=kLoop, calls=%fused_computation.41 | loop fusion | bytes 393216 | tf_op jit(solution)/shard_map/slice | solution.py:449
  1.9 2.4 %collective-permute-start = (bf16[64,2,384]{2,1,0:T(2,128)(2,1)S(1)}, bf16[64,2,384]{2,1,0:T(2,128)(2,1)S(1)}, u32[]{:S(2)}, u32[]{:S(2)}) collective-permute-start(bf16[64,2,384]{2,1,0:T(2,128)(2,1)S(1)} %get-tuple-element.17), channel_id=1, source_target_pairs={{0,1},{1,2},{2,3},{4,5},{5,6},{6,7},{8,9},{9,10},{10,11},{12,13},{... | collective-permute-start | bytes 294920 | tf_op jit(solution)/shard_map/ppermute | solution.py:26
  4.3 1.3 %collective-permute-start.1 = (bf16[64,2,384]{2,1,0:T(2,128)(2,1)S(1)}, bf16[64,2,384]{2,1,0:T(2,128)(2,1)S(1)}, u32[]{:S(2)}, u32[]{:S(2)}) collective-permute-start(bf16[64,2,384]{2,1,0:T(2,128)(2,1)S(1)} %get-tuple-element.18), channel_id=1, source_target_pairs={{1,0},{2,1},{3,2},{5,4},{6,5},{7,6},{9,8},{10,9},{11,10},{13,12},{... | collective-permute-start | bytes 294920 | tf_op jit(solution)/shard_map/ppermute | solution.py:26
  5.7 1.1 %fusion.10 = (bf16[2,128,384]{2,1,0:T(8,128)(2,1)S(1)}, bf16[2,128,384]{2,1,0:T(8,128)(2,1)S(1)}) fusion(bf16[64,128,384]{2,1,0:T(8,128)(2,1)} %pixels.1), kind=kLoop, calls=%fused_computation.40 | loop fusion | bytes 786432 | tf_op jit(solution)/shard_map/slice | solution.py:450
  6.8 0.1 select_convert_fusion.taps
  7.0 2.7 %collective-permute-done.1.right = bf16[64,2,384]{2,1,0:T(2,128)(2,1)S(1)} collective-permute-done((bf16[64,2,384]{2,1,0:T(2,128)(2,1)S(1)}, bf16[64,2,384]{2,1,0:T(2,128)(2,1)S(1)}, u32[]{:S(2)}, u32[]{:S(2)}) %collective-permute-start.1) | collective-permute-done | bytes 98336 | tf_op jit(solution)/shard_map/ppermute | solution.py:26
  9.7 3.4 %collective-permute-start.2 = (bf16[2,132,384]{2,1,0:T(8,128)(2,1)S(1)}, bf16[2,132,384]{2,1,0:T(8,128)(2,1)S(1)}, u32[]{:S(2)}, u32[]{:S(2)}) collective-permute-start(bf16[2,132,384]{2,1,0:T(8,128)(2,1)S(1)} %pad_maximum_fusion), channel_id=1, source_target_pairs={{0,4},{4,8},{8,12},{12,16},{16,20},{20,24},{24,28},{1,5},{5,9},{9,... | collective-permute-start | bytes 608264 | tf_op jit(solution)/shard_map/ppermute | solution.py:26
  13.1 1.3 %collective-permute-start.3 = (bf16[2,132,384]{2,1,0:T(8,128)(2,1)S(1)}, bf16[2,132,384]{2,1,0:T(8,128)(2,1)S(1)}, u32[]{:S(2)}, u32[]{:S(2)}) collective-permute-start(bf16[2,132,384]{2,1,0:T(8,128)(2,1)S(1)} %pad_maximum_fusion.1), channel_id=1, source_target_pairs={{4,0},{8,4},{12,8},{16,12},{20,16},{24,20},{28,24},{5,1},{9,5},{13... | collective-permute-start | bytes 608264 | tf_op jit(solution)/shard_map/ppermute | solution.py:26
  14.4 0.1 broadcast_in_dim.29.col_scale
  14.5 9.3 %smooth_inner.1 = (bf16[64,128,384]{2,1,0:T(8,128)(2,1)}, f32[256,256]{1,0:T(8,128)S(1)}, f32[384,256]{1,0:T(8,128)S(1)}, bf16[8,144,384]{2,1,0:T(8,128)(2,1)S(1)}) custom-call(bf16[64,128,384]{2,1,0:T(8,128)(2,1)} %pixels.1, bf16[64,2,384]{2,1,0:T(2,128)(2,1)S(1)} %collective-permute-done.left, bf16[64,2,384]{2,1,0:T(2,128)(2,1)S(1)} %collective-permute-done.1.right, ...), custom_call_target="tpu_custom_call" | custom-call | flops 10000000000 | bytes 30000000 | tf_op jit(solution)/shard_map/smooth_inner/pallas_call | solution.py:191
  23.8 0.0 copy-start
  23.8 1.6 %smooth_edges.1 = (bf16[4,128,384]{2,1,0:T(8,128)(2,1)S(1)}, f32[768,128]{1,0:T(8,128)S(1)}) custom-call(f32[64]{0:T(128)S(1)} %fusion.9.row_scale, bf16[2,132,384]{2,1,0:T(8,128)(2,1)S(1)} %collective-permute-done.2.above, bf16[2,132,384]{2,1,0:T(8,128)(2,1)S(1)} %collective-permute-done.3.below, bf16[8,144,384]{2,1,0:T(8,128)(2,1)S(1)} %get-tuple-element.9.kept, ...), custom_call_target="tpu_custom_call" | custom-call | flops 1000000000 | bytes 1000000 | tf_op jit(solution)/shard_map/smooth_edges/pallas_call | solution.py:212
  25.4 3.0 %collective-permute-start.4 = (f32[384,128]{1,0:T(8,128)S(1)}, f32[384,128]{1,0:T(8,128)S(1)}, u32[]{:S(2)}, u32[]{:S(2)}) collective-permute-start(f32[384,128]{1,0:T(8,128)S(1)} %constant_dynamic-slice_fusion), channel_id=1, source_target_pairs={{0,1},{1,0},{2,3},{3,2},{4,5},{5,4},{6,7},{7,6},{8,9},{9,8},{10,11... | collective-permute-start | bytes 589832 | tf_op jit(solution)/shard_map/ppermute | solution.py:247
  28.5 1.1 %collective-permute-done.4 = f32[384,128]{1,0:T(8,128)S(1)} collective-permute-done((f32[384,128]{1,0:T(8,128)S(1)}, f32[384,128]{1,0:T(8,128)S(1)}, u32[]{:S(2)}, u32[]{:S(2)}) %collective-permute-start.4) | collective-permute-done | bytes 196640 | tf_op jit(solution)/shard_map/ppermute | solution.py:247
  29.6 2.4 %collective-permute-start.5 = (f32[192,128]{1,0:T(8,128)S(1)}, f32[192,128]{1,0:T(8,128)S(1)}, u32[]{:S(2)}, u32[]{:S(2)}) collective-permute-start(f32[192,128]{1,0:T(8,128)S(1)} %get-tuple-element.21), channel_id=1, source_target_pairs={{0,4},{1,5},{2,6},{3,7},{4,0},{5,1},{6,2},{7,3},{8,12},{9,13},{10,... | collective-permute-start | bytes 294920 | tf_op jit(solution)/shard_map/ppermute | solution.py:255
  32.0 1.6 %collective-permute-start.9 = (f32[192,128]{1,0:T(8,128)S(1)}, f32[192,128]{1,0:T(8,128)S(1)}, u32[]{:S(2)}, u32[]{:S(2)}) collective-permute-start(f32[192,128]{1,0:T(8,128)S(1)} %get-tuple-element.22), channel_id=1, source_target_pairs={{0,8},{1,9},{2,10},{3,11},{4,12},{5,13},{6,14},{7,15},{8,0},{9,1},... | collective-permute-start | bytes 294920 | tf_op jit(solution)/shard_map/ppermute | solution.py:256
  33.6 1.8 %collective-permute-done.5 = f32[192,128]{1,0:T(8,128)S(1)} collective-permute-done((f32[192,128]{1,0:T(8,128)S(1)}, f32[192,128]{1,0:T(8,128)S(1)}, u32[]{:S(2)}, u32[]{:S(2)}) %collective-permute-start.5) | collective-permute-done | bytes 98336 | tf_op jit(solution)/shard_map/ppermute | solution.py:255
  35.3 1.5 %collective-permute-done.9 = f32[192,128]{1,0:T(8,128)S(1)} collective-permute-done((f32[192,128]{1,0:T(8,128)S(1)}, f32[192,128]{1,0:T(8,128)S(1)}, u32[]{:S(2)}, u32[]{:S(2)}) %collective-permute-start.9) | collective-permute-done | bytes 98336 | tf_op jit(solution)/shard_map/ppermute | solution.py:256
  36.8 0.6 collective-permute-start.6
  37.5 2.6 %collective-permute-start.10 = (f32[192,128]{1,0:T(8,128)S(1)}, f32[192,128]{1,0:T(8,128)S(1)}, u32[]{:S(2)}, u32[]{:S(2)}) collective-permute-start(f32[192,128]{1,0:T(8,128)S(1)} %get-tuple-element.20), channel_id=1, source_target_pairs={{0,16},{1,17},{2,18},{3,19},{4,20},{5,21},{6,22},{7,23},{8,24},{9,... | collective-permute-start | bytes 294920 | tf_op jit(solution)/shard_map/ppermute | solution.py:256
  40.0 1.5 %collective-permute-done.6 = f32[192,128]{1,0:T(8,128)S(1)} collective-permute-done((f32[192,128]{1,0:T(8,128)S(1)}, f32[192,128]{1,0:T(8,128)S(1)}, u32[]{:S(2)}, u32[]{:S(2)}) %collective-permute-start.6) | collective-permute-done | bytes 98336 | tf_op jit(solution)/shard_map/ppermute | solution.py:255
  41.5 1.6 %collective-permute-start.7 = (f32[192,128]{1,0:T(8,128)S(1)}, f32[192,128]{1,0:T(8,128)S(1)}, u32[]{:S(2)}, u32[]{:S(2)}) collective-permute-start(f32[192,128]{1,0:T(8,128)S(1)} %add.257), channel_id=1, source_target_pairs={{0,8},{1,9},{2,10},{3,11},{4,12},{5,13},{6,14},{7,15},{8,0},{9,1},... | collective-permute-start | bytes 294920 | tf_op jit(solution)/shard_map/ppermute | solution.py:255
  43.2 1.5 %collective-permute-start.11 = (f32[192,128]{1,0:T(8,128)S(1)}, f32[192,128]{1,0:T(8,128)S(1)}, u32[]{:S(2)}, u32[]{:S(2)}) collective-permute-start(f32[192,128]{1,0:T(8,128)S(1)} %add.261), channel_id=1, source_target_pairs={{0,4},{1,5},{2,6},{3,7},{4,0},{5,1},{6,2},{7,3},{8,12},{9,13},{10,... | collective-permute-start | bytes 294920 | tf_op jit(solution)/shard_map/ppermute | solution.py:256
  44.7 1.5 %collective-permute-done.7 = f32[192,128]{1,0:T(8,128)S(1)} collective-permute-done((f32[192,128]{1,0:T(8,128)S(1)}, f32[192,128]{1,0:T(8,128)S(1)}, u32[]{:S(2)}, u32[]{:S(2)}) %collective-permute-start.7) | collective-permute-done | bytes 98336 | tf_op jit(solution)/shard_map/ppermute | solution.py:255
  46.2 2.6 %collective-permute-start.8 = (f32[192,128]{1,0:T(8,128)S(1)}, f32[192,128]{1,0:T(8,128)S(1)}, u32[]{:S(2)}, u32[]{:S(2)}) collective-permute-start(f32[192,128]{1,0:T(8,128)S(1)} %add.258), channel_id=1, source_target_pairs={{0,16},{1,17},{2,18},{3,19},{4,20},{5,21},{6,22},{7,23},{8,24},{9,... | collective-permute-start | bytes 294920 | tf_op jit(solution)/shard_map/ppermute | solution.py:255
  48.9 0.8 %collective-permute-start.12 = (f32[192,128]{1,0:T(8,128)S(1)}, f32[192,128]{1,0:T(8,128)S(1)}, u32[]{:S(2)}, u32[]{:S(2)}) collective-permute-start(f32[192,128]{1,0:T(8,128)S(1)} %add.262), channel_id=1, source_target_pairs={{0,2},{1,3},{2,0},{3,1},{4,6},{5,7},{6,4},{7,5},{8,10},{9,11},{10,... | collective-permute-start | bytes 294920 | tf_op jit(solution)/shard_map/ppermute | solution.py:256
  49.7 2.1 %collective-permute-done.8 = f32[192,128]{1,0:T(8,128)S(1)} collective-permute-done((f32[192,128]{1,0:T(8,128)S(1)}, f32[192,128]{1,0:T(8,128)S(1)}, u32[]{:S(2)}, u32[]{:S(2)}) %collective-permute-start.8) | collective-permute-done | bytes 98336 | tf_op jit(solution)/shard_map/ppermute | solution.py:255
  51.8 1.7 %collective-permute-done.12 = f32[192,128]{1,0:T(8,128)S(1)} collective-permute-done((f32[192,128]{1,0:T(8,128)S(1)}, f32[192,128]{1,0:T(8,128)S(1)}, u32[]{:S(2)}, u32[]{:S(2)}) %collective-permute-start.12) | collective-permute-done | bytes 98336 | tf_op jit(solution)/shard_map/ppermute | solution.py:256
  53.6 0.1 collective-permute-start.13
  53.7 0.1 copy.5.start
  53.8 1.3 %collective-permute-done.13 = f32[384,128]{1,0:T(8,128)S(1)} collective-permute-done((f32[384,128]{1,0:T(8,128)S(1)}, f32[384,128]{1,0:T(8,128)S(1)}, u32[]{:S(2)}, u32[]{:S(2)}) %collective-permute-start.13) | collective-permute-done | bytes 196640 | tf_op jit(solution)/shard_map/ppermute | solution.py:260
  55.1 15.7 %components.1 = (f32[384]{0:T(512)}, f32[384,384]{1,0:T(8,128)}, f32[64,64,128]{2,1,0:T(8,128)}) custom-call(f32[768,128]{1,0:T(8,128)S(1)} %maximum_select_fusion.packed, f32[384,64]{1,0:T(8,128)S(1)} %copy.5.start, bf16[4,128,384]{2,1,0:T(8,128)(2,1)S(1)} %get-tuple-element.13.edge_rows, bf16[64,128,384]{2,1,0:T(8,128)(2,1)} %get-tuple-element.14.smooth_hbm), custom_call_target="tpu_custom_call" | custom-call | flops 1000000000 | bytes 10000000 | tf_op jit(solution)/shard_map/components/pallas_call | solution.py:419
  (27 shorter events, 0.3 us)
Async XLA Ops:
  1.9 5.0 %collective-permute-start = (bf16[64,2,384]{2,1,0:T(2,128)(2,1)S(1)}, bf16[64,2,384]{2,1,0:T(2,128)(2,1)S(1)}, u32[]{:S(2)}, u32[]{:S(2)}) collective-permute-start(bf16[64,2,384]{2,1,0:T(2,128)(2,1)S(1)} %get-tuple-element.17), channel_id=1, source_target_pairs={{0,1},{1,2},{2,3},{4,5},{5,6},{6,7},{8,9},{9,10},{10,11},{12,13},{... | collective-permute-start | bytes 294920 | tf_op jit(solution)/shard_map/ppermute | solution.py:26
  4.3 5.3 %collective-permute-start.1 = (bf16[64,2,384]{2,1,0:T(2,128)(2,1)S(1)}, bf16[64,2,384]{2,1,0:T(2,128)(2,1)S(1)}, u32[]{:S(2)}, u32[]{:S(2)}) collective-permute-start(bf16[64,2,384]{2,1,0:T(2,128)(2,1)S(1)} %get-tuple-element.18), channel_id=1, source_target_pairs={{1,0},{2,1},{3,2},{5,4},{6,5},{7,6},{9,8},{10,9},{11,10},{13,12},{... | collective-permute-start | bytes 294920 | tf_op jit(solution)/shard_map/ppermute | solution.py:26
  9.7 14.1 %collective-permute-start.2 = (bf16[2,132,384]{2,1,0:T(8,128)(2,1)S(1)}, bf16[2,132,384]{2,1,0:T(8,128)(2,1)S(1)}, u32[]{:S(2)}, u32[]{:S(2)}) collective-permute-start(bf16[2,132,384]{2,1,0:T(8,128)(2,1)S(1)} %pad_maximum_fusion), channel_id=1, source_target_pairs={{0,4},{4,8},{8,12},{12,16},{16,20},{20,24},{24,28},{1,5},{5,9},{9,... | collective-permute-start | bytes 608264 | tf_op jit(solution)/shard_map/ppermute | solution.py:26
  13.1 10.7 %collective-permute-start.3 = (bf16[2,132,384]{2,1,0:T(8,128)(2,1)S(1)}, bf16[2,132,384]{2,1,0:T(8,128)(2,1)S(1)}, u32[]{:S(2)}, u32[]{:S(2)}) collective-permute-start(bf16[2,132,384]{2,1,0:T(8,128)(2,1)S(1)} %pad_maximum_fusion.1), channel_id=1, source_target_pairs={{4,0},{8,4},{12,8},{16,12},{20,16},{24,20},{28,24},{5,1},{9,5},{13... | collective-permute-start | bytes 608264 | tf_op jit(solution)/shard_map/ppermute | solution.py:26
  23.8 29.9 %copy-start = (f32[384,64]{0,1:T(8,128)S(1)}, f32[384,64]{0,1:T(8,128)}, u32[]{:S(2)}) copy-start(f32[384,64]{0,1:T(8,128)} %param.3) | copy-start | bytes 294916
  25.4 4.1 %collective-permute-start.4 = (f32[384,128]{1,0:T(8,128)S(1)}, f32[384,128]{1,0:T(8,128)S(1)}, u32[]{:S(2)}, u32[]{:S(2)}) collective-permute-start(f32[384,128]{1,0:T(8,128)S(1)} %constant_dynamic-slice_fusion), channel_id=1, source_target_pairs={{0,1},{1,0},{2,3},{3,2},{4,5},{5,4},{6,7},{7,6},{8,9},{9,8},{10,11... | collective-permute-start | bytes 589832 | tf_op jit(solution)/shard_map/ppermute | solution.py:247
  29.6 5.8 %collective-permute-start.5 = (f32[192,128]{1,0:T(8,128)S(1)}, f32[192,128]{1,0:T(8,128)S(1)}, u32[]{:S(2)}, u32[]{:S(2)}) collective-permute-start(f32[192,128]{1,0:T(8,128)S(1)} %get-tuple-element.21), channel_id=1, source_target_pairs={{0,4},{1,5},{2,6},{3,7},{4,0},{5,1},{6,2},{7,3},{8,12},{9,13},{10,... | collective-permute-start | bytes 294920 | tf_op jit(solution)/shard_map/ppermute | solution.py:255
  32.0 4.8 %collective-permute-start.9 = (f32[192,128]{1,0:T(8,128)S(1)}, f32[192,128]{1,0:T(8,128)S(1)}, u32[]{:S(2)}, u32[]{:S(2)}) collective-permute-start(f32[192,128]{1,0:T(8,128)S(1)} %get-tuple-element.22), channel_id=1, source_target_pairs={{0,8},{1,9},{2,10},{3,11},{4,12},{5,13},{6,14},{7,15},{8,0},{9,1},... | collective-permute-start | bytes 294920 | tf_op jit(solution)/shard_map/ppermute | solution.py:256
  36.8 4.7 %collective-permute-start.6 = (f32[192,128]{1,0:T(8,128)S(1)}, f32[192,128]{1,0:T(8,128)S(1)}, u32[]{:S(2)}, u32[]{:S(2)}) collective-permute-start(f32[192,128]{1,0:T(8,128)S(1)} %get-tuple-element.19), channel_id=1, source_target_pairs={{0,2},{1,3},{2,0},{3,1},{4,6},{5,7},{6,4},{7,5},{8,10},{9,11},{10,... | collective-permute-start | bytes 294920 | tf_op jit(solution)/shard_map/ppermute | solution.py:255
  37.5 5.7 %collective-permute-start.10 = (f32[192,128]{1,0:T(8,128)S(1)}, f32[192,128]{1,0:T(8,128)S(1)}, u32[]{:S(2)}, u32[]{:S(2)}) collective-permute-start(f32[192,128]{1,0:T(8,128)S(1)} %get-tuple-element.20), channel_id=1, source_target_pairs={{0,16},{1,17},{2,18},{3,19},{4,20},{5,21},{6,22},{7,23},{8,24},{9,... | collective-permute-start | bytes 294920 | tf_op jit(solution)/shard_map/ppermute | solution.py:256
  41.5 4.7 %collective-permute-start.7 = (f32[192,128]{1,0:T(8,128)S(1)}, f32[192,128]{1,0:T(8,128)S(1)}, u32[]{:S(2)}, u32[]{:S(2)}) collective-permute-start(f32[192,128]{1,0:T(8,128)S(1)} %add.257), channel_id=1, source_target_pairs={{0,8},{1,9},{2,10},{3,11},{4,12},{5,13},{6,14},{7,15},{8,0},{9,1},... | collective-permute-start | bytes 294920 | tf_op jit(solution)/shard_map/ppermute | solution.py:255
  43.2 5.7 %collective-permute-start.11 = (f32[192,128]{1,0:T(8,128)S(1)}, f32[192,128]{1,0:T(8,128)S(1)}, u32[]{:S(2)}, u32[]{:S(2)}) collective-permute-start(f32[192,128]{1,0:T(8,128)S(1)} %add.261), channel_id=1, source_target_pairs={{0,4},{1,5},{2,6},{3,7},{4,0},{5,1},{6,2},{7,3},{8,12},{9,13},{10,... | collective-permute-start | bytes 294920 | tf_op jit(solution)/shard_map/ppermute | solution.py:256
  46.2 5.6 %collective-permute-start.8 = (f32[192,128]{1,0:T(8,128)S(1)}, f32[192,128]{1,0:T(8,128)S(1)}, u32[]{:S(2)}, u32[]{:S(2)}) collective-permute-start(f32[192,128]{1,0:T(8,128)S(1)} %add.258), channel_id=1, source_target_pairs={{0,16},{1,17},{2,18},{3,19},{4,20},{5,21},{6,22},{7,23},{8,24},{9,... | collective-permute-start | bytes 294920 | tf_op jit(solution)/shard_map/ppermute | solution.py:255
  48.9 4.7 %collective-permute-start.12 = (f32[192,128]{1,0:T(8,128)S(1)}, f32[192,128]{1,0:T(8,128)S(1)}, u32[]{:S(2)}, u32[]{:S(2)}) collective-permute-start(f32[192,128]{1,0:T(8,128)S(1)} %add.262), channel_id=1, source_target_pairs={{0,2},{1,3},{2,0},{3,1},{4,6},{5,7},{6,4},{7,5},{8,10},{9,11},{10,... | collective-permute-start | bytes 294920 | tf_op jit(solution)/shard_map/ppermute | solution.py:256
  53.6 1.5 %collective-permute-start.13 = (f32[384,128]{1,0:T(8,128)S(1)}, f32[384,128]{1,0:T(8,128)S(1)}, u32[]{:S(2)}, u32[]{:S(2)}) collective-permute-start(f32[384,128]{1,0:T(8,128)S(1)} %pad_maximum_fusion.2), channel_id=1, source_target_pairs={{0,1},{1,0},{2,3},{3,2},{4,5},{5,4},{6,7},{7,6},{8,9},{9,8},{10,11... | collective-permute-start | bytes 589832 | tf_op jit(solution)/shard_map/ppermute | solution.py:260

commit v2 on v1

--- a/solution.py
+++ b/solution.py
@@ -43,7 +43,7 @@
     place = jnp.where(beside < 2 * WIDTH, place, -count)
     taps = jnp.zeros((count, count + HALO_ROWS), jnp.float32)
     for offset in range(5):
-        taps = jnp.where(place == out + offset - 2, GAUSS[offset], taps)
+        taps = jnp.where(place == out + offset - 2, GAUSS[0] * GAUSS[offset], taps)
     return taps.astype(jnp.bfloat16)
 
 
@@ -93,7 +93,7 @@
 
     def vertical(g, i):
         at = slice(i * strip, (i + 1) * strip)
-        scale = col_scale[at, :] * GAUSS[0]
+        scale = col_scale[at, :] if i in (0, group - 1) else None
         for f in range(feat // LANES):
             lanes = slice(f * LANES, (f + 1) * LANES)
             held = []
@@ -105,7 +105,7 @@
                         break
                     v, held[k] = v + held[k], v
                 else:
-                    v = (v * scale).astype(jnp.bfloat16)
+                    v = (v if scale is None else v * scale).astype(jnp.bfloat16)
                     smooth[g * group + WIDTH + r - 4, at, lanes] = v
 
     fetch(0).wait()
@@ -449,7 +449,7 @@
     left, right = edges("col", pixels[:, :WIDTH], pixels[:, tile_cols - WIDTH :])
     wider = lambda rows: jnp.concatenate([pixels[rows], left[rows], right[rows]], axis=1)
     row_edges = edges("row", wider(slice(0, WIDTH)), wider(slice(tile_rows - WIDTH, tile_rows)))
-    row_scale = GAUSS[0] / edge_weight(lax.axis_index("row") * tile_rows, tile_rows, rows_total)
+    row_scale = 1.0 / edge_weight(lax.axis_index("row") * tile_rows, tile_rows, rows_total)
     col_scale = 1.0 / edge_weight(lax.axis_index("col") * tile_cols, tile_cols, cols_total)
     col_scale = jnp.broadcast_to(col_scale[:, None], (tile_cols, LANES))
     smoothed, edge_rows, packed = smooth_and_gram(

time: 71.2 us -> 70.7 us (level)
  transfers between devices with their start and end apart: 14 -> 14, of which waited for: 9 -> 9; matrix products, arithmetic and copies ran while one was open for 2% -> 2% of each run, Pallas kernels for 13% -> 12%
where the time goes in v2:
time: 70.7 us; the launch traced here: 70.5 us
  Pallas kernels  26 us (37%)
  starting transfers between devices  25.2 us (36%)
  waiting for transfers between devices  15.2 us (21%)
  local copies, waits for them, and re-layouts  2.6 us (4%)
  between operations  1.07 us (2%)
    pallas_call x1, Pallas kernels, components(): pl.pallas_call(functools.partial(components_kernel, count), out_shape=(ja...  15.7 us
    pallas_call x1, Pallas kernels, smooth_and_gram(): pl.pallas_call(inner_kernel, out_shape=(pltpu.HBM(pixels.shape, jnp.bfloa...  8.74 us
    ppermute x4, starting transfers between devices, edges(): return (lax.ppermute(last, axis, up), lax.ppermute(first, axis, down))  8.39 us
    ppermute x4, starting transfers between devices, all_sum(): got_a = lax.ppermute(a, axes, first)  7.33 us
    ppermute x4, waiting for transfers between devices, all_sum(): got_a = lax.ppermute(a, axes, first)  6.92 us
    ppermute x4, starting transfers between devices, all_sum(): got_b = lax.ppermute(b, axes, second)  6.42 us
    ppermute x4, waiting for transfers between devices, all_sum(): got_b = lax.ppermute(b, axes, second)  3.21 us
    ppermute x1, starting transfers between devices, all_sum(): kept = mine + lax.ppermute(other, axes, core)  3.03 us
  transfers between devices with their start and end apart: 14, of which 9 were waited for; matrix products, arithmetic and copies ran while one was open for 2% of the time, Pallas kernels for 12%

profile of v2, /device:TPU:0, one launch (start us, length us, event | category | flops | bytes accessed | tf_op | source)
XLA Modules:
  0.0 70.5 jit_solution(11410492409357683631)
XLA Ops:
  0.6 1.3 %fusion.11 = (bf16[64,2,384]{2,1,0:T(2,128)(2,1)S(1)}, bf16[64,2,384]{2,1,0:T(2,128)(2,1)S(1)}) fusion(bf16[64,128,384]{2,1,0:T(8,128)(2,1)} %pixels.1), kind=kLoop, calls=%fused_computation.41 | loop fusion | bytes 393216 | tf_op jit(solution)/shard_map/slice | solution.py:449
  1.9 2.4 %collective-permute-start = (bf16[64,2,384]{2,1,0:T(2,128)(2,1)S(1)}, bf16[64,2,384]{2,1,0:T(2,128)(2,1)S(1)}, u32[]{:S(2)}, u32[]{:S(2)}) collective-permute-start(bf16[64,2,384]{2,1,0:T(2,128)(2,1)S(1)} %get-tuple-element.17), channel_id=1, source_target_pairs={{0,1},{1,2},{2,3},{4,5},{5,6},{6,7},{8,9},{9,10},{10,11},{12,13},{... | collective-permute-start | bytes 294920 | tf_op jit(solution)/shard_map/ppermute | solution.py:26
  4.3 1.3 %collective-permute-start.1 = (bf16[64,2,384]{2,1,0:T(2,128)(2,1)S(1)}, bf16[64,2,384]{2,1,0:T(2,128)(2,1)S(1)}, u32[]{:S(2)}, u32[]{:S(2)}) collective-permute-start(bf16[64,2,384]{2,1,0:T(2,128)(2,1)S(1)} %get-tuple-element.18), channel_id=1, source_target_pairs={{1,0},{2,1},{3,2},{5,4},{6,5},{7,6},{9,8},{10,9},{11,10},{13,12},{... | collective-permute-start | bytes 294920 | tf_op jit(solution)/shard_map/ppermute | solution.py:26
  5.7 1.1 %fusion.10 = (bf16[2,128,384]{2,1,0:T(8,128)(2,1)S(1)}, bf16[2,128,384]{2,1,0:T(8,128)(2,1)S(1)}) fusion(bf16[64,128,384]{2,1,0:T(8,128)(2,1)} %pixels.1), kind=kLoop, calls=%fused_computation.40 | loop fusion | bytes 786432 | tf_op jit(solution)/shard_map/slice | solution.py:450
  6.8 0.1 select_convert_fusion.taps
  7.0 2.7 %collective-permute-done.1.right = bf16[64,2,384]{2,1,0:T(2,128)(2,1)S(1)} collective-permute-done((bf16[64,2,384]{2,1,0:T(2,128)(2,1)S(1)}, bf16[64,2,384]{2,1,0:T(2,128)(2,1)S(1)}, u32[]{:S(2)}, u32[]{:S(2)}) %collective-permute-start.1) | collective-permute-done | bytes 98336 | tf_op jit(solution)/shard_map/ppermute | solution.py:26
  9.7 3.4 %collective-permute-start.2 = (bf16[2,132,384]{2,1,0:T(8,128)(2,1)S(1)}, bf16[2,132,384]{2,1,0:T(8,128)(2,1)S(1)}, u32[]{:S(2)}, u32[]{:S(2)}) collective-permute-start(bf16[2,132,384]{2,1,0:T(8,128)(2,1)S(1)} %pad_maximum_fusion), channel_id=1, source_target_pairs={{0,4},{4,8},{8,12},{12,16},{16,20},{20,24},{24,28},{1,5},{5,9},{9,... | collective-permute-start | bytes 608264 | tf_op jit(solution)/shard_map/ppermute | solution.py:26
  13.1 1.3 %collective-permute-start.3 = (bf16[2,132,384]{2,1,0:T(8,128)(2,1)S(1)}, bf16[2,132,384]{2,1,0:T(8,128)(2,1)S(1)}, u32[]{:S(2)}, u32[]{:S(2)}) collective-permute-start(bf16[2,132,384]{2,1,0:T(8,128)(2,1)S(1)} %pad_maximum_fusion.1), channel_id=1, source_target_pairs={{4,0},{8,4},{12,8},{16,12},{20,16},{24,20},{28,24},{5,1},{9,5},{13... | collective-permute-start | bytes 608264 | tf_op jit(solution)/shard_map/ppermute | solution.py:26
  14.4 0.1 broadcast_in_dim.29.col_scale
  14.5 8.7 %smooth_inner.1 = (bf16[64,128,384]{2,1,0:T(8,128)(2,1)}, f32[256,256]{1,0:T(8,128)S(1)}, f32[384,256]{1,0:T(8,128)S(1)}, bf16[8,144,384]{2,1,0:T(8,128)(2,1)S(1)}) custom-call(bf16[64,128,384]{2,1,0:T(8,128)(2,1)} %pixels.1, bf16[64,2,384]{2,1,0:T(2,128)(2,1)S(1)} %collective-permute-done.left, bf16[64,2,384]{2,1,0:T(2,128)(2,1)S(1)} %collective-permute-done.1.right, ...), custom_call_target="tpu_custom_call" | custom-call | flops 10000000000 | bytes 30000000 | tf_op jit(solution)/shard_map/smooth_inner/pallas_call | solution.py:191
  23.3 0.0 copy-start
  23.3 1.6 %smooth_edges.1 = (bf16[4,128,384]{2,1,0:T(8,128)(2,1)S(1)}, f32[768,128]{1,0:T(8,128)S(1)}) custom-call(f32[64]{0:T(128)S(1)} %fusion.9.row_scale, bf16[2,132,384]{2,1,0:T(8,128)(2,1)S(1)} %collective-permute-done.2.above, bf16[2,132,384]{2,1,0:T(8,128)(2,1)S(1)} %collective-permute-done.3.below, bf16[8,144,384]{2,1,0:T(8,128)(2,1)S(1)} %get-tuple-element.9.kept, ...), custom_call_target="tpu_custom_call" | custom-call | flops 1000000000 | bytes 1000000 | tf_op jit(solution)/shard_map/smooth_edges/pallas_call | solution.py:212
  24.9 3.0 %collective-permute-start.4 = (f32[384,128]{1,0:T(8,128)S(1)}, f32[384,128]{1,0:T(8,128)S(1)}, u32[]{:S(2)}, u32[]{:S(2)}) collective-permute-start(f32[384,128]{1,0:T(8,128)S(1)} %constant_dynamic-slice_fusion), channel_id=1, source_target_pairs={{0,1},{1,0},{2,3},{3,2},{4,5},{5,4},{6,7},{7,6},{8,9},{9,8},{10,11... | collective-permute-start | bytes 589832 | tf_op jit(solution)/shard_map/ppermute | solution.py:247
  27.9 1.1 %collective-permute-done.4 = f32[384,128]{1,0:T(8,128)S(1)} collective-permute-done((f32[384,128]{1,0:T(8,128)S(1)}, f32[384,128]{1,0:T(8,128)S(1)}, u32[]{:S(2)}, u32[]{:S(2)}) %collective-permute-start.4) | collective-permute-done | bytes 196640 | tf_op jit(solution)/shard_map/ppermute | solution.py:247
  29.1 2.4 %collective-permute-start.5 = (f32[192,128]{1,0:T(8,128)S(1)}, f32[192,128]{1,0:T(8,128)S(1)}, u32[]{:S(2)}, u32[]{:S(2)}) collective-permute-start(f32[192,128]{1,0:T(8,128)S(1)} %get-tuple-element.21), channel_id=1, source_target_pairs={{0,4},{1,5},{2,6},{3,7},{4,0},{5,1},{6,2},{7,3},{8,12},{9,13},{10,... | collective-permute-start | bytes 294920 | tf_op jit(solution)/shard_map/ppermute | solution.py:255
  31.5 1.6 %collective-permute-start.9 = (f32[192,128]{1,0:T(8,128)S(1)}, f32[192,128]{1,0:T(8,128)S(1)}, u32[]{:S(2)}, u32[]{:S(2)}) collective-permute-start(f32[192,128]{1,0:T(8,128)S(1)} %get-tuple-element.22), channel_id=1, source_target_pairs={{0,8},{1,9},{2,10},{3,11},{4,12},{5,13},{6,14},{7,15},{8,0},{9,1},... | collective-permute-start | bytes 294920 | tf_op jit(solution)/shard_map/ppermute | solution.py:256
  33.0 1.8 %collective-permute-done.5 = f32[192,128]{1,0:T(8,128)S(1)} collective-permute-done((f32[192,128]{1,0:T(8,128)S(1)}, f32[192,128]{1,0:T(8,128)S(1)}, u32[]{:S(2)}, u32[]{:S(2)}) %collective-permute-start.5) | collective-permute-done | bytes 98336 | tf_op jit(solution)/shard_map/ppermute | solution.py:255
  34.8 1.5 %collective-permute-done.9 = f32[192,128]{1,0:T(8,128)S(1)} collective-permute-done((f32[192,128]{1,0:T(8,128)S(1)}, f32[192,128]{1,0:T(8,128)S(1)}, u32[]{:S(2)}, u32[]{:S(2)}) %collective-permute-start.9) | collective-permute-done | bytes 98336 | tf_op jit(solution)/shard_map/ppermute | solution.py:256
  36.3 0.6 collective-permute-start.6
  36.9 2.6 %collective-permute-start.10 = (f32[192,128]{1,0:T(8,128)S(1)}, f32[192,128]{1,0:T(8,128)S(1)}, u32[]{:S(2)}, u32[]{:S(2)}) collective-permute-start(f32[192,128]{1,0:T(8,128)S(1)} %get-tuple-element.20), channel_id=1, source_target_pairs={{0,16},{1,17},{2,18},{3,19},{4,20},{5,21},{6,22},{7,23},{8,24},{9,... | collective-permute-start | bytes 294920 | tf_op jit(solution)/shard_map/ppermute | solution.py:256
  39.5 1.5 %collective-permute-done.6 = f32[192,128]{1,0:T(8,128)S(1)} collective-permute-done((f32[192,128]{1,0:T(8,128)S(1)}, f32[192,128]{1,0:T(8,128)S(1)}, u32[]{:S(2)}, u32[]{:S(2)}) %collective-permute-start.6) | collective-permute-done | bytes 98336 | tf_op jit(solution)/shard_map/ppermute | solution.py:255
  41.0 1.6 %collective-permute-start.7 = (f32[192,128]{1,0:T(8,128)S(1)}, f32[192,128]{1,0:T(8,128)S(1)}, u32[]{:S(2)}, u32[]{:S(2)}) collective-permute-start(f32[192,128]{1,0:T(8,128)S(1)} %add.257), channel_id=1, source_target_pairs={{0,8},{1,9},{2,10},{3,11},{4,12},{5,13},{6,14},{7,15},{8,0},{9,1},... | collective-permute-start | bytes 294920 | tf_op jit(solution)/shard_map/ppermute | solution.py:255
  42.6 1.5 %collective-permute-start.11 = (f32[192,128]{1,0:T(8,128)S(1)}, f32[192,128]{1,0:T(8,128)S(1)}, u32[]{:S(2)}, u32[]{:S(2)}) collective-permute-start(f32[192,128]{1,0:T(8,128)S(1)} %add.261), channel_id=1, source_target_pairs={{0,4},{1,5},{2,6},{3,7},{4,0},{5,1},{6,2},{7,3},{8,12},{9,13},{10,... | collective-permute-start | bytes 294920 | tf_op jit(solution)/shard_map/ppermute | solution.py:256
  44.2 1.5 %collective-permute-done.7 = f32[192,128]{1,0:T(8,128)S(1)} collective-permute-done((f32[192,128]{1,0:T(8,128)S(1)}, f32[192,128]{1,0:T(8,128)S(1)}, u32[]{:S(2)}, u32[]{:S(2)}) %collective-permute-start.7) | collective-permute-done | bytes 98336 | tf_op jit(solution)/shard_map/ppermute | solution.py:255
  45.7 2.6 %collective-permute-start.8 = (f32[192,128]{1,0:T(8,128)S(1)}, f32[192,128]{1,0:T(8,128)S(1)}, u32[]{:S(2)}, u32[]{:S(2)}) collective-permute-start(f32[192,128]{1,0:T(8,128)S(1)} %add.258), channel_id=1, source_target_pairs={{0,16},{1,17},{2,18},{3,19},{4,20},{5,21},{6,22},{7,23},{8,24},{9,... | collective-permute-start | bytes 294920 | tf_op jit(solution)/shard_map/ppermute | solution.py:255
  48.4 0.8 %collective-permute-start.12 = (f32[192,128]{1,0:T(8,128)S(1)}, f32[192,128]{1,0:T(8,128)S(1)}, u32[]{:S(2)}, u32[]{:S(2)}) collective-permute-start(f32[192,128]{1,0:T(8,128)S(1)} %add.262), channel_id=1, source_target_pairs={{0,2},{1,3},{2,0},{3,1},{4,6},{5,7},{6,4},{7,5},{8,10},{9,11},{10,... | collective-permute-start | bytes 294920 | tf_op jit(solution)/shard_map/ppermute | solution.py:256
  49.1 2.2 %collective-permute-done.8 = f32[192,128]{1,0:T(8,128)S(1)} collective-permute-done((f32[192,128]{1,0:T(8,128)S(1)}, f32[192,128]{1,0:T(8,128)S(1)}, u32[]{:S(2)}, u32[]{:S(2)}) %collective-permute-start.8) | collective-permute-done | bytes 98336 | tf_op jit(solution)/shard_map/ppermute | solution.py:255
  51.3 1.7 %collective-permute-done.12 = f32[192,128]{1,0:T(8,128)S(1)} collective-permute-done((f32[192,128]{1,0:T(8,128)S(1)}, f32[192,128]{1,0:T(8,128)S(1)}, u32[]{:S(2)}, u32[]{:S(2)}) %collective-permute-start.12) | collective-permute-done | bytes 98336 | tf_op jit(solution)/shard_map/ppermute | solution.py:256
  53.1 0.1 collective-permute-start.13
  53.2 0.1 copy.5.start
  53.3 1.3 %collective-permute-done.13 = f32[384,128]{1,0:T(8,128)S(1)} collective-permute-done((f32[384,128]{1,0:T(8,128)S(1)}, f32[384,128]{1,0:T(8,128)S(1)}, u32[]{:S(2)}, u32[]{:S(2)}) %collective-permute-start.13) | collective-permute-done | bytes 196640 | tf_op jit(solution)/shard_map/ppermute | solution.py:260
  54.6 15.7 %components.1 = (f32[384]{0:T(512)}, f32[384,384]{1,0:T(8,128)}, f32[64,64,128]{2,1,0:T(8,128)}) custom-call(f32[768,128]{1,0:T(8,128)S(1)} %maximum_select_fusion.packed, f32[384,64]{1,0:T(8,128)S(1)} %copy.5.start, bf16[4,128,384]{2,1,0:T(8,128)(2,1)S(1)} %get-tuple-element.13.edge_rows, bf16[64,128,384]{2,1,0:T(8,128)(2,1)} %get-tuple-element.14.smooth_hbm), custom_call_target="tpu_custom_call" | custom-call | flops 1000000000 | bytes 10000000 | tf_op jit(solution)/shard_map/components/pallas_call | solution.py:419
  (27 shorter events, 0.3 us)
Async XLA Ops:
  1.9 5.0 %collective-permute-start = (bf16[64,2,384]{2,1,0:T(2,128)(2,1)S(1)}, bf16[64,2,384]{2,1,0:T(2,128)(2,1)S(1)}, u32[]{:S(2)}, u32[]{:S(2)}) collective-permute-start(bf16[64,2,384]{2,1,0:T(2,128)(2,1)S(1)} %get-tuple-element.17), channel_id=1, source_target_pairs={{0,1},{1,2},{2,3},{4,5},{5,6},{6,7},{8,9},{9,10},{10,11},{12,13},{... | collective-permute-start | bytes 294920 | tf_op jit(solution)/shard_map/ppermute | solution.py:26
  4.3 5.3 %collective-permute-start.1 = (bf16[64,2,384]{2,1,0:T(2,128)(2,1)S(1)}, bf16[64,2,384]{2,1,0:T(2,128)(2,1)S(1)}, u32[]{:S(2)}, u32[]{:S(2)}) collective-permute-start(bf16[64,2,384]{2,1,0:T(2,128)(2,1)S(1)} %get-tuple-element.18), channel_id=1, source_target_pairs={{1,0},{2,1},{3,2},{5,4},{6,5},{7,6},{9,8},{10,9},{11,10},{13,12},{... | collective-permute-start | bytes 294920 | tf_op jit(solution)/shard_map/ppermute | solution.py:26
  9.7 13.6 %collective-permute-start.2 = (bf16[2,132,384]{2,1,0:T(8,128)(2,1)S(1)}, bf16[2,132,384]{2,1,0:T(8,128)(2,1)S(1)}, u32[]{:S(2)}, u32[]{:S(2)}) collective-permute-start(bf16[2,132,384]{2,1,0:T(8,128)(2,1)S(1)} %pad_maximum_fusion), channel_id=1, source_target_pairs={{0,4},{4,8},{8,12},{12,16},{16,20},{20,24},{24,28},{1,5},{5,9},{9,... | collective-permute-start | bytes 608264 | tf_op jit(solution)/shard_map/ppermute | solution.py:26
  13.1 10.2 %collective-permute-start.3 = (bf16[2,132,384]{2,1,0:T(8,128)(2,1)S(1)}, bf16[2,132,384]{2,1,0:T(8,128)(2,1)S(1)}, u32[]{:S(2)}, u32[]{:S(2)}) collective-permute-start(bf16[2,132,384]{2,1,0:T(8,128)(2,1)S(1)} %pad_maximum_fusion.1), channel_id=1, source_target_pairs={{4,0},{8,4},{12,8},{16,12},{20,16},{24,20},{28,24},{5,1},{9,5},{13... | collective-permute-start | bytes 608264 | tf_op jit(solution)/shard_map/ppermute | solution.py:26
  23.3 29.9 %copy-start = (f32[384,64]{0,1:T(8,128)S(1)}, f32[384,64]{0,1:T(8,128)}, u32[]{:S(2)}) copy-start(f32[384,64]{0,1:T(8,128)} %param.3) | copy-start | bytes 294916
  24.9 4.1 %collective-permute-start.4 = (f32[384,128]{1,0:T(8,128)S(1)}, f32[384,128]{1,0:T(8,128)S(1)}, u32[]{:S(2)}, u32[]{:S(2)}) collective-permute-start(f32[384,128]{1,0:T(8,128)S(1)} %constant_dynamic-slice_fusion), channel_id=1, source_target_pairs={{0,1},{1,0},{2,3},{3,2},{4,5},{5,4},{6,7},{7,6},{8,9},{9,8},{10,11... | collective-permute-start | bytes 589832 | tf_op jit(solution)/shard_map/ppermute | solution.py:247
  29.1 5.8 %collective-permute-start.5 = (f32[192,128]{1,0:T(8,128)S(1)}, f32[192,128]{1,0:T(8,128)S(1)}, u32[]{:S(2)}, u32[]{:S(2)}) collective-permute-start(f32[192,128]{1,0:T(8,128)S(1)} %get-tuple-element.21), channel_id=1, source_target_pairs={{0,4},{1,5},{2,6},{3,7},{4,0},{5,1},{6,2},{7,3},{8,12},{9,13},{10,... | collective-permute-start | bytes 294920 | tf_op jit(solution)/shard_map/ppermute | solution.py:255
  31.5 4.8 %collective-permute-start.9 = (f32[192,128]{1,0:T(8,128)S(1)}, f32[192,128]{1,0:T(8,128)S(1)}, u32[]{:S(2)}, u32[]{:S(2)}) collective-permute-start(f32[192,128]{1,0:T(8,128)S(1)} %get-tuple-element.22), channel_id=1, source_target_pairs={{0,8},{1,9},{2,10},{3,11},{4,12},{5,13},{6,14},{7,15},{8,0},{9,1},... | collective-permute-start | bytes 294920 | tf_op jit(solution)/shard_map/ppermute | solution.py:256
  36.3 4.7 %collective-permute-start.6 = (f32[192,128]{1,0:T(8,128)S(1)}, f32[192,128]{1,0:T(8,128)S(1)}, u32[]{:S(2)}, u32[]{:S(2)}) collective-permute-start(f32[192,128]{1,0:T(8,128)S(1)} %get-tuple-element.19), channel_id=1, source_target_pairs={{0,2},{1,3},{2,0},{3,1},{4,6},{5,7},{6,4},{7,5},{8,10},{9,11},{10,... | collective-permute-start | bytes 294920 | tf_op jit(solution)/shard_map/ppermute | solution.py:255
  36.9 5.7 %collective-permute-start.10 = (f32[192,128]{1,0:T(8,128)S(1)}, f32[192,128]{1,0:T(8,128)S(1)}, u32[]{:S(2)}, u32[]{:S(2)}) collective-permute-start(f32[192,128]{1,0:T(8,128)S(1)} %get-tuple-element.20), channel_id=1, source_target_pairs={{0,16},{1,17},{2,18},{3,19},{4,20},{5,21},{6,22},{7,23},{8,24},{9,... | collective-permute-start | bytes 294920 | tf_op jit(solution)/shard_map/ppermute | solution.py:256
  41.0 4.7 %collective-permute-start.7 = (f32[192,128]{1,0:T(8,128)S(1)}, f32[192,128]{1,0:T(8,128)S(1)}, u32[]{:S(2)}, u32[]{:S(2)}) collective-permute-start(f32[192,128]{1,0:T(8,128)S(1)} %add.257), channel_id=1, source_target_pairs={{0,8},{1,9},{2,10},{3,11},{4,12},{5,13},{6,14},{7,15},{8,0},{9,1},... | collective-permute-start | bytes 294920 | tf_op jit(solution)/shard_map/ppermute | solution.py:255
  42.6 5.7 %collective-permute-start.11 = (f32[192,128]{1,0:T(8,128)S(1)}, f32[192,128]{1,0:T(8,128)S(1)}, u32[]{:S(2)}, u32[]{:S(2)}) collective-permute-start(f32[192,128]{1,0:T(8,128)S(1)} %add.261), channel_id=1, source_target_pairs={{0,4},{1,5},{2,6},{3,7},{4,0},{5,1},{6,2},{7,3},{8,12},{9,13},{10,... | collective-permute-start | bytes 294920 | tf_op jit(solution)/shard_map/ppermute | solution.py:256
  45.7 5.6 %collective-permute-start.8 = (f32[192,128]{1,0:T(8,128)S(1)}, f32[192,128]{1,0:T(8,128)S(1)}, u32[]{:S(2)}, u32[]{:S(2)}) collective-permute-start(f32[192,128]{1,0:T(8,128)S(1)} %add.258), channel_id=1, source_target_pairs={{0,16},{1,17},{2,18},{3,19},{4,20},{5,21},{6,22},{7,23},{8,24},{9,... | collective-permute-start | bytes 294920 | tf_op jit(solution)/shard_map/ppermute | solution.py:255
  48.4 4.7 %collective-permute-start.12 = (f32[192,128]{1,0:T(8,128)S(1)}, f32[192,128]{1,0:T(8,128)S(1)}, u32[]{:S(2)}, u32[]{:S(2)}) collective-permute-start(f32[192,128]{1,0:T(8,128)S(1)} %add.262), channel_id=1, source_target_pairs={{0,2},{1,3},{2,0},{3,1},{4,6},{5,7},{6,4},{7,5},{8,10},{9,11},{10,... | collective-permute-start | bytes 294920 | tf_op jit(solution)/shard_map/ppermute | solution.py:256
  53.1 1.5 %collective-permute-start.13 = (f32[384,128]{1,0:T(8,128)S(1)}, f32[384,128]{1,0:T(8,128)S(1)}, u32[]{:S(2)}, u32[]{:S(2)}) collective-permute-start(f32[384,128]{1,0:T(8,128)S(1)} %pad_maximum_fusion.2), channel_id=1, source_target_pairs={{0,1},{1,0},{2,3},{3,2},{4,5},{5,4},{6,7},{7,6},{8,9},{9,8},{10,11... | collective-permute-start | bytes 589832 | tf_op jit(solution)/shard_map/ppermute | solution.py:260
